TPU v7x, 256 devices: a whole 4x4x8 slice. The times are simulated.
256 devices in a mesh: blk: 64 (over y, z, core), sp: 4 (over x).
Axes of the slice: x: 4, y: 4, z: 8, core: 2. Of those that a mesh axis runs over, the one named last changes fastest.
Arguments:
- species: float32 [8, 2048, 4096], P('sp', 'blk'), may hold values from 0 to 0.25
- interface_normal_flow: float32 [3, 2048, 4096], P(None, 'blk'), may hold values from -6 to 6
- face_diffusion: float32 [3, 2048, 4096], P(None, 'blk'), may hold values from 0.3 to 3
- inv_volume: float32 [2048, 4096], P('blk'), may hold values from 0.5 to 2
- diffusivity: float32 [8], P('sp'), may hold values from 0.2 to 2
- low_partner: int32 [64, 64], P('blk'), may hold values from 0 to 63, as said below
- high_partner: int32 [64, 64], P('blk'), may hold values from 0 to 63, as said below
- low_orient: int32 [64, 64], P('blk'), may hold values from 0 to 7
- high_orient: int32 [64, 64], P('blk'), may hold values from 0 to 7, as said below
- droplet_table: float32 [65536, 128], P(('blk', 'sp')), may hold values from -6 to 6
- parcel_block: int32 [65536, 1], P(('blk', 'sp')), may hold values from 0 to 63; in each aligned block of 256 rows (0 to 255, 256 to 511, ...) at most 6 rows name the same one
- parcel_cell: int32 [65536], P(('blk', 'sp')), may hold values from 0 to 131071
- parcel_live: int32 [65536], P(('blk', 'sp')), may hold values 0 or 1
Outputs:
- new_species: float32 [8, 2048, 4096], P('sp', 'blk')
- arrived: float32 [98304, 128], P(('blk', 'sp'))
Inputs may be any that keep to these rules, and one draw needn't show every extreme that they name: low_partner: in each row no block appears more than 1 times and some block appears exactly 1 times; high_partner[c, t] = b exactly when low_partner[b, t] = c. high_partner: in each row no block appears more than 1 times and some block appears exactly 1 times. high_orient[c, t] = low_orient[high_partner[c, t], t]. parcel_block: among the slots of one device no block is named more than 6 times.
All inputs are finite; a program needn't handle non-finite values. No bound on the sum of `parcel_live` on one device may be relied on, other than what follows from the above.
Results may differ from a plain program's by a relative error of at most 0.00002.
Values sent between devices are 32-bit elements; how exact they have to be, the bound alone decides.
A program may use at most 192 MiB of HBM per device.

v0:
```python
import jax
import jax.numpy as jnp
from jax import lax
from jax.sharding import PartitionSpec as P

PV = 128
BJ = 64
BK = 64
TILE_SIDE = 8
TILES = 64


section_step = 0.5
friction_timescale = 0.3


def spread(value, axis, source):
    kept = jnp.where(lax.axis_index(axis) == source, value, 0).astype(value.dtype)
    return lax.psum(kept, axis)


def face_tiles(face):
    leading = face.shape[:-1]
    levels = len(leading)
    blocked = face.reshape(leading + (BJ // TILE_SIDE, TILE_SIDE, BK // TILE_SIDE, TILE_SIDE))
    axes_order = tuple(range(levels)) + (levels, levels + 2, levels + 1, levels + 3)
    return jnp.transpose(blocked, axes_order).reshape(leading + (TILES, TILE_SIDE * TILE_SIDE))


def tile_face(tiles):
    leading = tiles.shape[:-2]
    levels = len(leading)
    blocked = tiles.reshape(leading + (BJ // TILE_SIDE, BK // TILE_SIDE, TILE_SIDE, TILE_SIDE))
    axes_order = tuple(range(levels)) + (levels, levels + 2, levels + 1, levels + 3)
    return jnp.transpose(blocked, axes_order).reshape(leading + (BJ * BK,))


def orient(tiles, codes, inverse):
    square = tiles.reshape(tiles.shape[:-1] + (TILE_SIDE, TILE_SIDE))
    selector = codes[..., None, None, None]
    transposed = selector // 4 % 2 == 1
    flip_rows = selector % 2 == 1
    flip_columns = selector // 2 % 2 == 1
    if not inverse:
        square = jnp.where(transposed, jnp.swapaxes(square, -1, -2), square)
    square = jnp.where(flip_rows, jnp.flip(square, -2), square)
    square = jnp.where(flip_columns, jnp.flip(square, -1), square)
    if inverse:
        square = jnp.where(transposed, jnp.swapaxes(square, -1, -2), square)
    return square.reshape(tiles.shape)


def droplet_motion_update(droplet_table, evaporate_component, ambient_flow_speed, alive_indicator):
    boiled_off_quantity = (
        jax.nn.softplus(droplet_table[:, 1])
        * (jax.nn.sigmoid(droplet_table[:, 2]) - evaporate_component)
        * alive_indicator
    )
    shifted_droplet_list = droplet_table.at[:, 0].add(-boiled_off_quantity)
    shifted_droplet_list = shifted_droplet_list.at[:, 3:6].add(
        friction_timescale * (jnp.transpose(ambient_flow_speed) - droplet_table[:, 3:6])
    )
    return (boiled_off_quantity, shifted_droplet_list * alive_indicator[:, None])


def matched_rank(targets, blocks):
    onehot = (targets[:, None] == jnp.arange(blocks)[None, :]).astype(jnp.int32)
    return jnp.sum((jnp.cumsum(onehot, axis=0) - onehot) * onehot, axis=1)


def face_flux(velocity, diffusion, scaled, difference, middle, weight):
    return velocity * middle - diffusion * (scaled * difference - middle * weight)


def body(
    species,
    interface_normal_flow,
    face_diffusion,
    inv_volume,
    diffusivity,
    low_partner,
    high_partner,
    low_orient,
    high_orient,
    droplet_table,
    parcel_block,
    parcel_cell,
    parcel_live,
):
    blocks = lax.axis_size("blk")
    layers = species.shape[1]
    local_species = species.shape[0]
    low_face = jnp.concatenate(
        [species[:, 0], interface_normal_flow[0:1, 0], face_diffusion[0:1, 0]], axis=0
    )
    low_pack = jnp.transpose(face_tiles(low_face), (1, 0, 2))
    high_pack = jnp.transpose(face_tiles(species[:, layers - 1]), (1, 0, 2))
    low_source = low_partner[0]
    high_source = high_partner[0]
    tile_cap = max(1, TILES // blocks)
    low_rank = matched_rank(low_source, blocks)
    high_rank = matched_rank(high_source, blocks)
    send_high = (
        jnp.zeros((blocks, tile_cap) + high_pack.shape[1:], jnp.float32)
        .at[high_source, high_rank]
        .set(high_pack)
    )
    send_low = (
        jnp.zeros((blocks, tile_cap) + low_pack.shape[1:], jnp.float32)
        .at[low_source, low_rank]
        .set(low_pack)
    )
    got_high, got_low = (
        lax.all_to_all(send_high, "blk", split_axis=0, concat_axis=0, tiled=True),
        lax.all_to_all(send_low, "blk", split_axis=0, concat_axis=0, tiled=True),
    )
    picked_high = got_high[low_source, low_rank]
    picked_low = got_low[high_source, high_rank]
    ghost_low = tile_face(jnp.transpose(orient(picked_high, low_orient[0], False), (1, 0, 2)))
    ghost_high = tile_face(jnp.transpose(orient(picked_low, high_orient[0], True), (1, 0, 2)))
    parcel_rows = droplet_table.shape[0]
    parcel_cap = 3 * parcel_rows // (2 * blocks)
    target_block = parcel_block[:, 0]
    active_rows = parcel_live == 1
    onehot = ((target_block[:, None] == jnp.arange(blocks)[None, :]) & active_rows[:, None]).astype(
        jnp.int32
    )
    rank_before = jnp.sum((jnp.cumsum(onehot, axis=0) - onehot) * onehot, axis=1)
    slot_index = jnp.where(
        active_rows, target_block * parcel_cap + rank_before, blocks * parcel_cap
    )
    send_rows = (
        jnp.zeros((blocks * parcel_cap, PV), jnp.float32)
        .at[slot_index]
        .set(droplet_table, mode="drop")
        .reshape(blocks, parcel_cap, PV)
    )
    send_cells = (
        jnp.zeros((blocks * parcel_cap,), jnp.int32)
        .at[slot_index]
        .set(parcel_cell, mode="drop")
        .reshape(blocks, parcel_cap)
    )
    send_flags = (
        jnp.zeros((blocks * parcel_cap,), jnp.int32)
        .at[slot_index]
        .set(parcel_live, mode="drop")
        .reshape(blocks, parcel_cap)
    )
    got_rows, got_cells, received_flags = (
        lax.all_to_all(send_rows, "blk", split_axis=0, concat_axis=0, tiled=True),
        lax.all_to_all(send_cells, "blk", split_axis=0, concat_axis=0, tiled=True),
        lax.all_to_all(send_flags, "blk", split_axis=0, concat_axis=0, tiled=True),
    )
    inbound_droplet_list = got_rows.reshape(blocks * parcel_cap, PV)
    landing_grid_points = got_cells.reshape(-1)
    alive_indicator = received_flags.reshape(-1).astype(jnp.float32)
    fuel_local = species[0].reshape(-1)
    fuel_field = spread(fuel_local, "sp", 0)
    evaporate_component = fuel_field[landing_grid_points]
    ambient_flow_speed = interface_normal_flow.reshape(3, -1)[:, landing_grid_points]
    boiled_off_quantity, shifted_droplet_list = droplet_motion_update(
        inbound_droplet_list, evaporate_component, ambient_flow_speed, alive_indicator
    )
    source = (
        jnp.zeros((layers * BJ * BK,), jnp.float32).at[landing_grid_points].add(boiled_off_quantity)
    )
    total_source = lax.psum(source, "sp").reshape(layers, BJ * BK)
    scaled_face = diffusivity[:, None]
    scaled_field = diffusivity[:, None, None]
    ghost_top = ghost_high[:local_species]
    bottom_layer = species[:, 0]
    top_layer = species[:, layers - 1]
    bottom_diff = bottom_layer - ghost_low
    bottom_mean = 0.5 * (bottom_layer + ghost_low)
    inner_diff = species[:, 1:] - species[:, :-1]
    inner_mean = 0.5 * (species[:, 1:] + species[:, :-1])
    top_diff = ghost_top - top_layer
    top_mean = 0.5 * (ghost_top + top_layer)
    previous_row = jnp.roll(species, BK, axis=-1)
    previous_column = jnp.roll(species, 1, axis=-1)
    row_diff = species - previous_row
    row_mean = 0.5 * (species + previous_row)
    column_diff = species - previous_column
    column_mean = 0.5 * (species + previous_column)
    partial_terms = (
        jnp.sum(scaled_face * bottom_diff, axis=0),
        jnp.sum(scaled_field * inner_diff, axis=0),
        jnp.sum(scaled_face * top_diff, axis=0),
        jnp.sum(scaled_field * row_diff, axis=0),
        jnp.sum(scaled_field * column_diff, axis=0),
    )
    weight_bottom, weight_inner, weight_top, weight_row, weight_column = lax.psum(
        (partial_terms[0], partial_terms[1], partial_terms[2], partial_terms[3], partial_terms[4]),
        "sp",
    )
    flux_bottom = face_flux(
        interface_normal_flow[0, 0],
        face_diffusion[0, 0],
        scaled_face,
        bottom_diff,
        bottom_mean,
        weight_bottom,
    )
    flux_inner = face_flux(
        interface_normal_flow[0, 1:],
        face_diffusion[0, 1:],
        scaled_field,
        inner_diff,
        inner_mean,
        weight_inner,
    )
    flux_top = face_flux(
        ghost_high[local_species],
        ghost_high[local_species + 1],
        scaled_face,
        top_diff,
        top_mean,
        weight_top,
    )
    cell_index = jnp.arange(BJ * BK)
    wall_rows = cell_index // BK == 0
    wall_columns = cell_index % BK == 0
    flux_row = jnp.where(
        wall_rows,
        0.0,
        face_flux(
            interface_normal_flow[1],
            face_diffusion[1],
            scaled_field,
            row_diff,
            row_mean,
            weight_row,
        ),
    )
    flux_column = jnp.where(
        wall_columns,
        0.0,
        face_flux(
            interface_normal_flow[2],
            face_diffusion[2],
            scaled_field,
            column_diff,
            column_mean,
            weight_column,
        ),
    )
    divergence = (
        jnp.roll(flux_row, -BK, axis=-1)
        - flux_row
        + (jnp.roll(flux_column, -1, axis=-1) - flux_column)
    )
    divergence = divergence.at[:, : layers - 1].add(flux_inner)
    divergence = divergence.at[:, 1:].add(-flux_inner)
    divergence = divergence.at[:, 0].add(-flux_bottom)
    divergence = divergence.at[:, layers - 1].add(flux_top)
    global_index = lax.axis_index("sp") * local_species + jnp.arange(local_species)
    is_fuel = (global_index == 0).astype(jnp.float32)[:, None, None]
    tendency = inv_volume * (total_source * (is_fuel - species) - divergence)
    new_species = species + section_step * tendency
    return (new_species, shifted_droplet_list)


def solution(mesh):
    placed = (
        P("sp", "blk", None),
        P(None, "blk", None),
        P(None, "blk", None),
        P("blk", None),
        P("sp"),
        P("blk", None),
        P("blk", None),
        P("blk", None),
        P("blk", None),
        P(("blk", "sp"), None),
        P(("blk", "sp"), None),
        P(("blk", "sp")),
        P(("blk", "sp")),
    )
    return jax.shard_map(
        body,
        mesh=mesh,
        in_specs=placed,
        out_specs=(P("sp", "blk", None), P(("blk", "sp"), None)),
        check_vma=False,
    )
```

profile of v0, /device:TPU:2, one launch (start us, length us, event | category | flops | bytes accessed | tf_op | source)
XLA Modules:
  0.0 274.9 jit_solution(6906714011957227903)
XLA Ops:
  7.2 0.8 fusion.62
  10.2 0.8 fusion.17
  11.7 1.6 scatter_custom_fusion
  13.2 0.8 all_to_all.21
  14.0 12.1 %all-to-all-start = ((s32[64,1,6]{2,1,0:T(1,128)}), s32[64,1,6]{2,1,0:T(1,128)S(1)}, u32[]{:S(2)}, u32[]{:S(2)}) async-start(s32[64,1,6]{2,1,0:T(1,128)} %bitcast.4), calls=%async_computation | async-start | bytes 65536 | tf_op jit(solution)/shard_map/all_to_all | solution.py:152
  26.1 1.1 select_bitcast_fusion
  27.2 0.9 copy.152
  28.2 0.8 copy.144
  29.8 2.9 %slice_bitcast_fusion.1 = (f32[32,4096]{1,0:T(8,128)}, f32[32,4096]{1,0:T(8,128)}, f32[32,4096]{1,0:T(8,128)}, f32[32,4096]{1,0:T(8,128)}) fusion(f32[3,32,4096]{2,1,0:T(8,128)} %param.27, f32[3,32,4096]{2,1,0:T(8,128)} %param.26), kind=kLoop, calls=%fused_computation.31 | loop fusion | flops 262144 | bytes 4194304 | tf_op jit(solution)/shard_map/mul | solution.py:72
  32.7 2.3 slice_bitcast_fusion
  35.0 1.6 slice_multiply_fusion.1
  36.6 2.7 fusion.58
  39.3 1.1 concatenate.52
  40.6 0.9 concatenate.54
  43.8 1.2 maximum_bitcast_fusion
  45.1 5.2 %fusion.57 = (f32[32,4096]{1,0:T(8,128)}, f32[32,4096]{1,0:T(8,128)}) fusion(f32[2,32,4095]{2,0,1:T(2,128)S(1)} %bitcast.189, f32[2,32,1]{2,0,1:T(2,128)S(1)} %slice.289, f32[2]{0:T(128)S(1)} %copy-done.25, f32[2,32,4096]{2,1,0:T(8,128)S(1)} %copy-done, f32[2,32,4032]{2,0,1:T(2,128)S(1)} %bitcast.190, f32[2,32,64]{2,0,1:T(2,128)S(1)} %slice.285), kind=kLoop, calls=%fused_computation.177 | loop fusion | flops 1835008 | bytes 4194312 | tf_op jit(solution)/shard_map/reduce_sum | solution.py:191
  50.8 1.5 scatter_custom_fusion.2
  52.4 32.0 %copy.147 = f32[3,32,4096]{0,2,1:T(8,128)} copy(f32[3,32,4096]{2,1,0:T(8,128)} %param.26) | data formatting | bytes 3145728 | tf_op args[1]
  84.3 1.7 scatter_custom_fusion.1
  87.5 1.2 copy.137
  88.7 1.5 reshape.821
  90.4 2.4 scatter_fusion.1
  92.8 0.8 reshape.953
  94.3 2.4 scatter_fusion
  98.8 10.3 %all-to-all-start.2 = ((s32[64,1,6]{2,1,0:T(1,128)}), s32[64,1,6]{2,1,0:T(1,128)S(1)}, u32[]{:S(2)}, u32[]{:S(2)}) async-start(s32[64,1,6]{2,1,0:T(1,128)} %bitcast.5), calls=%async_computation.2 | async-start | bytes 65536 | tf_op jit(solution)/shard_map/all_to_all | solution.py:153
  110.6 8.1 %all-to-all-done.2 = s32[64,1,6]{2,1,0:T(1,128)S(1)} async-done(((s32[64,1,6]{2,1,0:T(1,128)}), s32[64,1,6]{2,1,0:T(1,128)S(1)}, u32[]{:S(2)}, u32[]{:S(2)}) %all-to-all-start.2) | async-done | bytes 1568 | tf_op jit(solution)/shard_map/all_to_all | solution.py:153
  118.7 4.6 %all-to-all-start.3 = ((f32[64,1,128]{2,1,0:T(1,128)}), f32[64,1,128]{2,1,0:T(1,128)S(1)}, u32[]{:S(2)}, u32[]{:S(2)}) async-start(f32[64,1,128]{2,1,0:T(1,128)} %reshape.951), calls=%async_computation.3 | async-start | bytes 65536 | tf_op jit(solution)/shard_map/all_to_all | solution.py:114
  123.3 0.8 convert_element_type.48
  124.3 10.4 %gather_fusion.3 = f32[384,3]{1,0:T(8,128)} fusion(f32[3,131072]{0,1:T(8,128)} %bitcast.46, s32[1024]{0:T(1024)S(1)} %pad_clamp_fusion), kind=kCustom, calls=%fused_computation.3 | custom fusion | bytes 10752 | tf_op jit(solution)/shard_map/gather | solution.py:161
  134.8 10.3 %all-to-all-start.4 = ((f32[64,1,256]{2,1,0:T(1,128)}), f32[64,1,256]{2,1,0:T(1,128)S(1)}, u32[]{:S(2)}, u32[]{:S(2)}) async-start(f32[64,1,256]{2,1,0:T(1,128)} %reshape.953), calls=%async_computation.4 | async-start | bytes 131072 | tf_op jit(solution)/shard_map/all_to_all | solution.py:115
  147.3 7.6 %all-to-all-done.4 = f32[64,1,256]{2,1,0:T(1,128)S(1)} async-done(((f32[64,1,256]{2,1,0:T(1,128)}), f32[64,1,256]{2,1,0:T(1,128)S(1)}, u32[]{:S(2)}, u32[]{:S(2)}) %all-to-all-start.4) | async-done | bytes 65568 | tf_op jit(solution)/shard_map/all_to_all | solution.py:115
  154.8 5.5 %all-to-all-start.1 = ((f32[64,6,128]{2,1,0:T(8,128)}), f32[64,6,128]{2,1,0:T(8,128)}, u32[]{:S(2)}, u32[]{:S(2)}) async-start(f32[64,6,128]{2,1,0:T(8,128)} %reshape.813), calls=%async_computation.1 | async-start | bytes 524288 | tf_op jit(solution)/shard_map/all_to_all | solution.py:151
  160.5 1.0 reshape.818
  161.5 1.1 copy.135
  162.9 0.9 reshape.819
  163.9 0.8 reduce.52
  165.6 6.5 %all-to-all-done.1 = f32[64,6,128]{2,1,0:T(8,128)} async-done(((f32[64,6,128]{2,1,0:T(8,128)}), f32[64,6,128]{2,1,0:T(8,128)}, u32[]{:S(2)}, u32[]{:S(2)}) %all-to-all-start.1) | async-done | bytes 196640 | tf_op jit(solution)/shard_map/all_to_all | solution.py:151
  172.1 1.0 reshape.814
  173.1 11.0 %gather_fusion = f32[384]{0:T(512)S(1)} fusion(f32[131072]{0:T(1024)} %all-reduce.5.cloned.1.call-done, s32[1024]{0:T(1024)S(1)} %pad_clamp_fusion), kind=kCustom, calls=%fused_computation | custom fusion | bytes 4608 | tf_op jit(solution)/shard_map/gather | solution.py:160
  184.2 1.6 fusion.21
  185.7 3.6 %scatter_custom_fusion.3 = f32[131072]{0:T(1024)S(1)} fusion(s32[384]{0:T(512)S(1)} %fusion.39, f32[384]{0:T(512)S(1)} %fusion.38, f32[]{:T(128)} %constant.290.clone.1), kind=kCustom, calls=%fused_computation.42 | custom fusion | flops 384 | bytes 524292 | tf_op jit(solution)/shard_map/scatter-add | solution.py:166
  189.4 0.9 mul.324
  191.0 1.3 reshape.909
  192.3 2.6 copy.143
  194.9 2.0 fusion.60
  196.8 1.7 reduce_sum.88
  198.6 0.9 slice.264
  199.5 1.1 slice_multiply_fusion
  200.6 0.7 mul.387
  201.3 0.7 mul.390
  202.1 15.5 %all-reduce = (f32[4096]{0:T(1024)S(1)}, f32[4096]{0:T(1024)S(1)}) all-reduce(f32[4096]{0:T(1024)S(1)} %fusion.25, f32[4096]{0:T(1024)S(1)} %copy-done.19), channel_id=1, replica_groups=mesh['blk'=64,'sp'=4] {'sp'}, use_global_device_ids=true, to_apply=%region_21.22 | all-reduce | flops 8192 | bytes 65536 | tf_op jit(solution)/shard_map/psum | solution.py:193
  218.9 1.8 add_select_fusion
  220.7 1.2 scatter-add.43
  221.9 1.5 broadcast_multiply_fusion.3
  223.4 27.7 %all-reduce.7.cloned.1.call-done = (f32[32,4096]{1,0:T(8,128)}, f32[32,4096]{1,0:T(8,128)}, f32[31,4096]{1,0:T(8,128)}, f32[32,4096]{1,0:T(8,128)}) async-done(((f32[32,4096]{1,0:T(8,128)}, f32[32,4096]{1,0:T(8,128)}, f32[31,4096]{1,0:T(8,128)}, f32[32,4096]{1,0:T(8,128)}), (f32[32,4096]{1,0:T(8,128)}, f32[32,4096]{1,0:T(8,128)}, f32[31,4096]{1,0:T(8,128)}, ...) | async-done | bytes 2080784 | tf_op jit(solution)/shard_map/psum | solution.py:193
  251.1 1.4 broadcast_multiply_fusion.1
  252.6 4.3 %subtract_select_fusion = (f32[2,32,4096]{2,0,1:T(2,128)S(1)}, f32[2,32,4096]{2,0,1:T(2,128)S(1)}) fusion(pred[4096]{0:T(1024)(128)(4,1)S(1)} %copy-done.30, f32[32,4096]{1,0:T(8,128)S(1)} %get-tuple-element.128, f32[32,4096]{1,0:T(8,128)S(1)} %copy-done.2, f32[32,4096]{1,0:T(8,128)S(1)} %copy-done.5, f32[2,32,4095]{2,0,1:T(2,128)S(1)} %bitcast.191, ...), kind=kLoop, calls=%fused_computation.17 | loop fusion | flops 5242880 | bytes 8396808 | tf_op jit(solution)/shard_map/jit(_where)/select_n | solution.py:236
  256.9 1.2 slice.287
  258.1 1.2 slice.291
  259.4 1.9 fusion
  261.3 2.1 fusion.2
  263.4 1.1 fusion.1
  264.8 1.7 multiply_add_fusion
  266.5 1.6 copy.148
  (166 shorter events, 18.9 us)
Async XLA Ops:
  7.2 21.0 %copy-start = (f32[2,32,4096]{2,1,0:T(8,128)S(1)}, f32[2,32,4096]{2,1,0:T(8,128)}, u32[]{:S(2)}) copy-start(f32[2,32,4096]{2,1,0:T(8,128)} %param.25) | copy-start | bytes 3145732
  11.7 14.5 %copy-start.40 = (s32[256]{0:T(256)}, s32[256]{0:T(256)S(1)}, u32[]{:S(2)}) copy-start(s32[256]{0:T(256)S(1)} %compare_select_fusion.3) | copy-start | bytes 3076
  14.0 84.9 %all-to-all-start = ((s32[64,1,6]{2,1,0:T(1,128)}), s32[64,1,6]{2,1,0:T(1,128)S(1)}, u32[]{:S(2)}, u32[]{:S(2)}) async-start(s32[64,1,6]{2,1,0:T(1,128)} %bitcast.4), calls=%async_computation | async-start | bytes 65536 | tf_op jit(solution)/shard_map/all_to_all | solution.py:152
  26.1 147.1 %all-reduce.5.cloned.1.call-start = ((), (), s32[]{:S(2)}) async-start(), calls=%async_computation.5 | async-start | bytes 1048576 | tf_op jit(solution)/shard_map/psum | solution.py:19
  29.1 16.0 %copy-start.13 = (f32[2,32,64]{2,0,1:T(2,128)}, f32[2,32,64]{2,0,1:T(2,128)S(1)}, u32[]{:S(2)}) copy-start(f32[2,32,64]{2,0,1:T(2,128)S(1)} %slice.285) | copy-start | bytes 49156
  29.2 15.9 %copy-start.15 = (f32[2,32,1]{2,0,1:T(2,128)}, f32[2,32,1]{2,0,1:T(2,128)S(1)}, u32[]{:S(2)}) copy-start(f32[2,32,1]{2,0,1:T(2,128)S(1)} %slice.289) | copy-start | bytes 772
  32.7 3.9 %copy-start.25 = (f32[2]{0:T(128)S(1)}, f32[2]{0:T(128)}, u32[]{:S(2)}) copy-start(f32[2]{0:T(128)} %param.29) | copy-start | bytes 28
  36.6 4.8 %copy-start.31 = (s32[1,64]{1,0:T(1,128)S(1)}, s32[1,64]{1,0:T(1,128)}, u32[]{:S(2)}) copy-start(s32[1,64]{1,0:T(1,128)} %param.30) | copy-start | bytes 772
  36.6 5.7 %copy-start.32 = (s32[1,64]{1,0:T(1,128)S(1)}, s32[1,64]{1,0:T(1,128)}, u32[]{:S(2)}) copy-start(s32[1,64]{1,0:T(1,128)} %param.31) | copy-start | bytes 772
  36.6 6.6 %copy-start.42 = (s32[1,64]{1,0:T(1,128)S(1)}, s32[1,64]{1,0:T(1,128)}, u32[]{:S(2)}) copy-start(s32[1,64]{1,0:T(1,128)} %param.32) | copy-start | bytes 772
  36.6 6.6 %copy-start.43 = (s32[1,64]{1,0:T(1,128)S(1)}, s32[1,64]{1,0:T(1,128)}, u32[]{:S(2)}) copy-start(s32[1,64]{1,0:T(1,128)} %param.33) | copy-start | bytes 772
  87.5 2.8 %copy-start.35 = (s32[64]{0:T(128)S(1)}, s32[64]{0:T(128)}, u32[]{:S(2)}) copy-start(s32[64]{0:T(128)} %get-tuple-element.115) | copy-start | bytes 772
  90.3 4.0 %copy-start.34 = (s32[64]{0:T(128)S(1)}, s32[64]{0:T(128)}, u32[]{:S(2)}) copy-start(s32[64]{0:T(128)} %get-tuple-element.114) | copy-start | bytes 772
  93.9 53.3 %copy-start.39 = (pred[64]{0:T(512)(128)(4,1)S(1)}, pred[64]{0:T(512)(128)(4,1)}, u32[]{:S(2)}) copy-start(pred[64]{0:T(512)(128)(4,1)} %get-tuple-element.122) | copy-start | bytes 196
  94.0 66.4 %copy-start.38 = (pred[64]{0:T(512)(128)(4,1)S(1)}, pred[64]{0:T(512)(128)(4,1)}, u32[]{:S(2)}) copy-start(pred[64]{0:T(512)(128)(4,1)} %get-tuple-element.120) | copy-start | bytes 196
  98.8 19.8 %all-to-all-start.2 = ((s32[64,1,6]{2,1,0:T(1,128)}), s32[64,1,6]{2,1,0:T(1,128)S(1)}, u32[]{:S(2)}, u32[]{:S(2)}) async-start(s32[64,1,6]{2,1,0:T(1,128)} %bitcast.5), calls=%async_computation.2 | async-start | bytes 65536 | tf_op jit(solution)/shard_map/all_to_all | solution.py:153
  118.7 16.1 %all-to-all-start.3 = ((f32[64,1,128]{2,1,0:T(1,128)}), f32[64,1,128]{2,1,0:T(1,128)S(1)}, u32[]{:S(2)}, u32[]{:S(2)}) async-start(f32[64,1,128]{2,1,0:T(1,128)} %reshape.951), calls=%async_computation.3 | async-start | bytes 65536 | tf_op jit(solution)/shard_map/all_to_all | solution.py:114
  124.3 61.4 %copy-start.28 = (f32[384]{0:T(512)}, f32[384]{0:T(512)S(1)}, u32[]{:S(2)}) copy-start(f32[384]{0:T(512)S(1)} %convert_element_type.43) | copy-start | bytes 4612
  134.8 20.1 %all-to-all-start.4 = ((f32[64,1,256]{2,1,0:T(1,128)}), f32[64,1,256]{2,1,0:T(1,128)S(1)}, u32[]{:S(2)}, u32[]{:S(2)}) async-start(f32[64,1,256]{2,1,0:T(1,128)} %reshape.953), calls=%async_computation.4 | async-start | bytes 131072 | tf_op jit(solution)/shard_map/all_to_all | solution.py:115
  154.8 17.3 %all-to-all-start.1 = ((f32[64,6,128]{2,1,0:T(8,128)}), f32[64,6,128]{2,1,0:T(8,128)}, u32[]{:S(2)}, u32[]{:S(2)}) async-start(f32[64,6,128]{2,1,0:T(8,128)} %reshape.813), calls=%async_computation.1 | async-start | bytes 524288 | tf_op jit(solution)/shard_map/all_to_all | solution.py:151
  160.3 90.8 %all-reduce.7.cloned.1.call-start = ((), (), s32[]{:S(2)}) async-start(), calls=%async_computation.6 | async-start | bytes 4194304 | tf_op jit(solution)/shard_map/psum | solution.py:193
  160.4 3.4 %copy-start.26 = (f32[2]{0:T(128)S(1)}, f32[2]{0:T(128)}, u32[]{:S(2)}) copy-start(f32[2]{0:T(128)} %param.29) | copy-start | bytes 28
  164.8 19.3 %copy-start.8 = (f32[384,1]{1,0:T(8,128)S(1)}, f32[384,1]{1,0:T(8,128)}, u32[]{:S(2)}) copy-start(f32[384,1]{1,0:T(8,128)} %convert_element_type.48) | copy-start | bytes 4612
  189.4 0.9 copy-start.33
  190.3 0.6 copy-start.37
  190.3 0.7 copy-start.36
  196.8 21.3 %copy-start.9 = (f32[384,1]{1,0:T(8,128)S(1)}, f32[384,1]{1,0:T(8,128)}, u32[]{:S(2)}) copy-start(f32[384,1]{1,0:T(8,128)} %get-tuple-element.112) | copy-start | bytes 4612
  199.5 2.6 copy-start.19
  220.6 31.8 %copy-start.2 = (f32[32,4096]{1,0:T(8,128)S(1)}, f32[32,4096]{1,0:T(8,128)}, u32[]{:S(2)}) copy-start(f32[32,4096]{1,0:T(8,128)} %get-tuple-element.102) | copy-start | bytes 1572868
  220.7 31.8 %copy-start.3 = (f32[32,4096]{1,0:T(8,128)S(1)}, f32[32,4096]{1,0:T(8,128)}, u32[]{:S(2)}) copy-start(f32[32,4096]{1,0:T(8,128)} %get-tuple-element.103) | copy-start | bytes 1572868
  221.8 30.6 %copy-start.14 = (f32[2,32,64]{2,0,1:T(2,128)S(1)}, f32[2,32,64]{2,0,1:T(2,128)}, u32[]{:S(2)}) copy-start(f32[2,32,64]{2,0,1:T(2,128)} %copy-done.13) | copy-start | bytes 49156
  221.9 30.6 %copy-start.16 = (f32[2,32,1]{2,0,1:T(2,128)S(1)}, f32[2,32,1]{2,0,1:T(2,128)}, u32[]{:S(2)}) copy-start(f32[2,32,1]{2,0,1:T(2,128)} %copy-done.15) | copy-start | bytes 772
  221.9 30.6 %copy-start.27 = (f32[2]{0:T(128)S(1)}, f32[2]{0:T(128)}, u32[]{:S(2)}) copy-start(f32[2]{0:T(128)} %param.29) | copy-start | bytes 28
  221.9 30.6 %copy-start.29 = (pred[4096]{0:T(1024)(128)(4,1)S(1)}, pred[4096]{0:T(1024)(128)(4,1)}, u32[]{:S(2)}) copy-start(pred[4096]{0:T(1024)(128)(4,1)} %get-tuple-element.132) | copy-start | bytes 12292
  221.9 30.6 %copy-start.30 = (pred[4096]{0:T(1024)(128)(4,1)S(1)}, pred[4096]{0:T(1024)(128)(4,1)}, u32[]{:S(2)}) copy-start(pred[4096]{0:T(1024)(128)(4,1)} %get-tuple-element.133) | copy-start | bytes 12292
  251.1 1.5 copy-start.4
  251.1 1.5 copy-start.5
  258.0 1.2 copy-start.12
  259.3 1.9 copy-start.1
  259.3 1.9 copy-start.6
  259.3 1.9 copy-start.7
  263.3 1.2 copy-start.17
  263.3 1.2 copy-start.22
  263.4 1.2 copy-start.23
  263.4 1.2 copy-start.24
  263.4 1.3 copy-start.18
  263.4 1.3 copy-start.20
  263.4 1.3 copy-start.21
  263.4 1.4 copy-start.10
  263.4 1.4 copy-start.11
  263.4 1.4 copy-start.41
Sparse Core Ops, SparseCore 0:
  29.3 48.2 all-reduce.4
  190.5 60.5 all-reduce.6
where the time goes:
time: 279 us; the launch traced here: 275 us
  local copies, waits for them, and re-layouts  98.2 us (35%)
  other arithmetic  53.4 us (19%)
  waiting for transfers between devices  49.9 us (18%)
  starting transfers between devices  42.9 us (15%)
  blocking collectives  15.5 us (6%)
  between operations  15.1 us (5%)
    unnamed x97, local copies, waits for them, and re-layouts  37.8 us
    psum x1, waiting for transfers between devices, body(): lax.psum((partial_terms[0], partial_terms[1], partial_terms[2], partial_t...  27.7 us
    psum x1, blocking collectives, body(): lax.psum((partial_terms[0], partial_terms[1], partial_terms[2], partial_t...  15.5 us
    all_to_all x1, starting transfers between devices, body(): lax.all_to_all(send_cells, 'blk', split_axis=0, concat_axis=0, tiled=True)  12.1 us
    gather x1, local copies, waits for them, and re-layouts, body(): evaporate_component = fuel_field[landing_grid_points]  11 us
    gather x1, local copies, waits for them, and re-layouts, body(): interface_normal_flow.reshape(3, -1)[:, landing_grid_points]  10.4 us
    all_to_all x1, starting transfers between devices, body(): lax.all_to_all(send_flags, 'blk', split_axis=0, concat_axis=0, tiled=True)  10.3 us
    all_to_all x1, starting transfers between devices, body(): lax.all_to_all(send_low, 'blk', split_axis=0, concat_axis=0, tiled=True)  10.3 us
  transfers between devices with their start and end apart: 7, of which 4 were waited for; matrix products, arithmetic and copies ran while one was open for 40% of the time, Pallas kernels for 0%

commit v1 on v0

v1 whole, which is shorter than its diff:
```python
import functools
import jax
import jax.numpy as jnp
import numpy as np
from jax import lax
from jax.experimental import pallas as pl
from jax.experimental.pallas import tpu as pltpu
from jax.sharding import PartitionSpec as P

NB = 64
NQ = 4
CAP = 6
LAYERS = 32
JK = 4096
MESH = pl.DeviceIdType.MESH
F32 = jnp.float32
BF16 = jnp.bfloat16
STEP = 0.5
DRAG = 0.3
VMEM_LIMIT = 48 * 1024 * 1024


def constants():
    lane = np.arange(512)
    cell = np.arange(64)
    pick = (lane[:, None] // 64 == cell[None, :] // 8) & (lane[:, None] % 8 == cell[None, :] % 8)
    r, c = cell // 8, cell % 8
    oriented, unoriented = [], []
    for code in range(8):
        f_row = (lambda v: 7 - v) if code & 1 else (lambda v: v)
        f_col = (lambda v: 7 - v) if code & 2 else (lambda v: v)
        r2, c2 = f_row(r), f_col(c)
        source = c2 * 8 + r2 if code & 4 else r2 * 8 + c2
        oriented += [cell[:, None] == source[None, :]] * 2
        source = f_row(c) * 8 + f_col(r) if code & 4 else f_row(r) * 8 + f_col(c)
        unoriented += [cell[:, None] == source[None, :]] * 2
    spread = np.zeros((128, 1024), bool)
    spread[:64, :512] = pick.T
    spread[64:, 512:] = pick.T
    asb = lambda m: jnp.asarray(m.astype(np.float32), BF16)
    return asb(pick), asb(np.concatenate(oriented, 1)), asb(np.concatenate(unoriented, 1)), asb(spread)


def pieces(x):
    hi = x.astype(BF16)
    rest = x - hi.astype(F32)
    mid = rest.astype(BF16)
    low = (rest - mid.astype(F32)).astype(BF16)
    return hi, mid, low


def mm(a, b):
    return lax.dot_general(a, b, (((1,), (0,)), ((), ())), preferred_element_type=F32)


def pick_rows(onehot, x):
    hi, mid, low = pieces(x)
    return (mm(onehot, hi) + mm(onehot, mid)) + mm(onehot, low)


def pick_lanes(x, onehot):
    hi, mid, low = pieces(x)
    return (mm(hi, onehot) + mm(mid, onehot)) + mm(low, onehot)


def iota(shape, axis):
    return lax.broadcasted_iota(jnp.int32, shape, axis)


def ones(mask):
    return jnp.where(mask, 1.0, 0.0).astype(BF16)


def column(row):
    n = row.shape[1]
    return jnp.sum(jnp.where(iota((n, n), 0) == iota((n, n), 1), row, 0.0), axis=1, keepdims=True)


def strip_mask():
    lane = iota((8, 512), 1)
    return (lane % 64) // 8 == iota((8, 512), 0)


def prep_kernel(
    dif, species, flow, diffusion, low_partner, high_partner, low_orient, high_orient,
    table, block, cell, live, pick, oriented, unoriented, msg_a, msg_b, z_part,
):
    d0, d1 = dif[0], dif[1]
    z_part[...] = d0 * species[0] + d1 * species[1]

    n = table.shape[0]
    alive = live[...] == 1
    target = block[...].astype(F32)
    key = jnp.where(alive, target, -1.0)
    key_col = column(key)
    same = key_col == key
    first, second = iota((n, n), 0), iota((n, n), 1)
    rank = jnp.sum(jnp.where(same & (first < second), 1.0, 0.0), axis=0, keepdims=True)
    rank_col = jnp.sum(jnp.where(same & (second < first), 1.0, 0.0), axis=1, keepdims=True)
    slot = jnp.where(alive, target * CAP + rank, -1.0)
    rows = table[...]
    place = ones(iota((NB * CAP, n), 0).astype(F32) == slot)
    msg_b[...] = pick_rows(place, rows)

    lane = iota((n, 128), 1)
    cell_col = column(cell[...].astype(F32))
    boil = jnp.maximum(rows, 0.0) + jnp.log1p(jnp.exp(-jnp.abs(rows)))
    sig = 1.0 / (1.0 + jnp.exp(-rows))
    kind = lane & 7
    meta = jnp.where(kind == 0, cell_col, jnp.where(kind == 1, boil[:, 1:2], jnp.where(kind == 2, sig[:, 2:3], jnp.where(kind == 3, 1.0, 0.0))))
    meta = jnp.where((lane >> 3).astype(F32) == rank_col, meta, 0.0)

    mask = strip_mask()
    faces = [
        species[0, LAYERS - 1 : LAYERS, :], species[1, LAYERS - 1 : LAYERS, :],
        species[0, 0:1, :], species[1, 0:1, :], flow[0, 0:1, :], diffusion[0, 0:1, :],
    ]
    strips = []
    for face in faces:
        for jt in range(8):
            strips.append(jnp.where(mask, face[:, jt * 512 : (jt + 1) * 512], 0.0))
    tiles = pick_lanes(jnp.concatenate(strips, axis=0), pick[...])
    turned = pick_lanes(tiles[:128], oriented[...])
    unturned = pick_lanes(tiles[128:], unoriented[...])
    high_code = column(high_orient[...].astype(F32))
    low_code = column(low_orient[...].astype(F32))

    def choose(x, code):
        out = x[:, :128]
        for o in range(1, 8):
            out = jnp.where(code == o, x[:, o * 128 : (o + 1) * 128], out)
        return out

    up0, up1 = (choose(turned[k * 64 : (k + 1) * 64], high_code) for k in range(2))
    lo0, lo1, fl, df = (choose(unturned[k * 64 : (k + 1) * 64], low_code) for k in range(4))
    left = iota((NB, 128), 1) < 64
    values = jnp.concatenate(
        [
            meta,
            jnp.where(left, up0, up1),
            jnp.where(left, lo0, lo1),
            jnp.where(left, fl, df),
            jnp.where(left, d0 * up0 + d1 * up1, 0.0),
            jnp.where(left, 0.0, d0 * lo0 + d1 * lo1),
        ],
        axis=0,
    )
    hp, lp = high_partner[...].astype(F32) * CAP, low_partner[...].astype(F32) * CAP
    keys = jnp.concatenate([jnp.where(alive, target * CAP, -1.0), hp + 2.0, lp + 3.0, lp + 4.0, hp + 1.0, lp + 1.0], axis=1)
    where_to = ones(iota((NB * CAP, keys.shape[1]), 0).astype(F32) == keys)
    msg_a[...] = pick_rows(where_to, values)


def exchange_kernel(msg_a, msg_b, z_part, recv_a, recv_b, z_sum, forward, z_got, z_mine, z_own, sems, recv_sems, wide_send, wide_recv, local_sems):
    b, q = lax.axis_index("blk"), lax.axis_index("sp")
    barrier = pltpu.get_barrier_semaphore()

    def greet(i, carry):
        pl.semaphore_signal(barrier, inc=1, device_id=(lax.rem(b + i, NB), q), device_id_type=MESH)
        return carry

    for d in range(1, NQ):
        pl.semaphore_signal(barrier, inc=1, device_id=(b, lax.rem(q + d, NQ)), device_id_type=MESH)
    lax.fori_loop(1, NB, greet, 0)
    own = pltpu.make_async_copy(z_part.at[q], z_own, local_sems.at[0])
    own.start()
    keep_a = pltpu.make_async_copy(msg_a.at[b], recv_a.at[b], local_sems.at[1])
    keep_b = pltpu.make_async_copy(msg_b.at[b], recv_b.at[b], local_sems.at[2])
    keep_a.start()
    keep_b.start()
    pl.semaphore_wait(barrier, NB + NQ - 2)

    def sp_copy(src, dst, k, d):
        return pltpu.make_async_remote_copy(
            src_ref=src, dst_ref=dst, send_sem=sems.at[k, d - 1], recv_sem=recv_sems.at[k, d - 1],
            device_id=(b, lax.rem(q + d, NQ)), device_id_type=MESH,
        )

    scatter = [sp_copy(z_part.at[lax.rem(q + d, NQ)], z_got.at[d - 1], 0, d) for d in range(1, NQ)]
    for copy in scatter:
        copy.start()

    def send(msg, recv, k):
        def step(i, carry):
            to = lax.rem(b + i, NB)
            pltpu.make_async_remote_copy(
                src_ref=msg.at[to], dst_ref=recv.at[b], send_sem=wide_send.at[k], recv_sem=wide_recv.at[k],
                device_id=(to, q), device_id_type=MESH,
            ).start()
            return carry

        lax.fori_loop(1, NB, step, 0)

    send(msg_a, recv_a, 0)
    send(msg_b, recv_b, 1)

    own.wait()
    for copy in scatter:
        copy.wait_recv()
    z_mine[...] = (z_own[...] + z_got[0]) + (z_got[1] + z_got[2])
    gather = [sp_copy(z_mine, z_sum.at[q], 1, d) for d in range(1, NQ)]
    for copy in gather:
        copy.start()
    keep_z = pltpu.make_async_copy(z_mine, z_sum.at[q], local_sems.at[3])
    keep_z.start()

    keep_a.wait()
    most = pl.ds(0, NB - 1)
    pltpu.make_async_copy(recv_a.at[most], recv_a.at[most], wide_recv.at[0]).wait()
    onward = [sp_copy(recv_a.at[:, 0], forward.at[q], 2, d) for d in range(1, NQ)]
    for copy in onward:
        copy.start()
    keep_f = pltpu.make_async_copy(recv_a.at[:, 0], forward.at[q], local_sems.at[4])
    keep_f.start()

    keep_b.wait()
    keep_z.wait()
    keep_f.wait()
    pltpu.make_async_copy(recv_b.at[most], recv_b.at[most], wide_recv.at[1]).wait()
    pltpu.make_async_copy(msg_a.at[most], msg_a.at[most], wide_send.at[0]).wait()
    pltpu.make_async_copy(msg_b.at[most], msg_b.at[most], wide_send.at[1]).wait()
    for copy in scatter:
        copy.wait_send()
    for copy in gather + onward:
        copy.wait()


def stack_field(ref_slice):
    return jnp.concatenate([ref_slice[:, i * 128 : (i + 1) * 128] for i in range(LAYERS)], axis=0)


def lookup(cells, field3):
    n = cells.shape[0]
    whole = cells.astype(jnp.int32)
    row = ((whole & 4095) >> 7) * LAYERS + (whole >> 12)
    got = mm(ones(iota((n, 1024), 1) == row), field3)
    got = (got[:, :128] + got[:, 128:256]) + got[:, 256:]
    return jnp.sum(jnp.where(iota((n, 128), 1) == (whole & 127), got, 0.0), axis=1, keepdims=True)


def fuel_kernel(forward, fuel, out):
    field3 = jnp.concatenate(pieces(stack_field(fuel[0])), axis=1)
    meta = forward[pl.ds(0, NB * NQ, stride=2), :]
    lane = iota((NB * NQ, 128), 1)
    found = jnp.zeros((NB * NQ, 128), F32)
    for r in range(CAP):
        found = jnp.where(lane == r, lookup(meta[:, 8 * r : 8 * r + 1], field3), found)
    out[...] = jnp.transpose(found)[:8]


def share_kernel(mine, out, sems, recv_sems, local_sem):
    b, q = lax.axis_index("blk"), lax.axis_index("sp")
    barrier = pltpu.get_barrier_semaphore()
    for d in range(1, NQ):
        pl.semaphore_signal(barrier, inc=1, device_id=(b, lax.rem(q + d, NQ)), device_id_type=MESH)
    pl.semaphore_wait(barrier, NQ - 1)

    @pl.when(q == 0)
    def _():
        keep = pltpu.make_async_copy(mine, out, local_sem)
        keep.start()
        copies = [
            pltpu.make_async_remote_copy(
                src_ref=mine, dst_ref=out, send_sem=sems.at[d - 1], recv_sem=recv_sems, device_id=(b, d), device_id_type=MESH
            )
            for d in range(1, NQ)
        ]
        for copy in copies:
            copy.start()
        for copy in copies:
            copy.wait_send()
        keep.wait()

    @pl.when(q != 0)
    def _():
        pltpu.make_async_copy(mine, out, recv_sems).wait()


def final_kernel(
    dif, species, flow, diffusion, inv_volume, z_sum, low_partner, high_partner,
    recv_a, recv_b, forward, found, spread, new_species, arrived, ghosts, source, fuel_col,
):
    q = lax.axis_index("sp")
    d = (dif[0], dif[1])
    left = iota((NB, 128), 1) < 64

    meta = forward[pl.ds(0, NB * NQ, stride=2), :]
    meta_t = jnp.transpose(meta)
    pad = jnp.concatenate([found[...], jnp.zeros((120, NB * NQ), F32)], axis=0)
    found_col = jnp.transpose(pad)
    fuel_col[...] = found_col
    lane = iota((NB * NQ, 128), 1)
    mass, cells = [], []
    for r in range(CAP):
        k = 8 * r
        gone = meta[:, k + 1 : k + 2] * (meta[:, k + 2 : k + 3] - found_col[:, r : r + 1])
        at = meta[:, k : k + 1].astype(jnp.int32) & 127
        mass.append(jnp.concatenate(pieces(jnp.where(lane == at, gone, 0.0)), axis=1))
        cells.append(meta_t[k : k + 1, :].astype(jnp.int32))
    mass = jnp.concatenate(mass, axis=0)
    cells = jnp.concatenate(cells, axis=1)
    row = ((cells & 4095) >> 7) * LAYERS + (cells >> 12)
    for m in range(4):
        hot = ones(iota((256, NB * NQ * CAP), 0) + m * 256 == row)
        part = mm(hot, mass)
        source[m * 256 : (m + 1) * 256, :] = (part[:, :128] + part[:, 128:256]) + part[:, 256:]

    own = recv_a[pl.ds(0, NB, stride=6), :]
    own_cells = jnp.concatenate([own[:, 8 * r : 8 * r + 1] for r in range(CAP)], axis=0)
    speeds = [lookup(own_cells, jnp.concatenate(pieces(stack_field(flow[k])), axis=1)) for k in range(3)]
    own_fuel = fuel_col[pl.ds(pl.multiple_of(q * NB, NB), NB), :]
    lane = iota((NB, 128), 1)
    keep = jnp.where((lane >= 3) & (lane <= 5), 1.0 - DRAG, 1.0)
    for r in range(CAP):
        k = 8 * r
        gone = own[:, k + 1 : k + 2] * (own[:, k + 2 : k + 3] - own_fuel[:, r : r + 1])
        drag = DRAG * own[:, k + 3 : k + 4]
        change = jnp.where(lane == 0, -gone, 0.0)
        for c in range(3):
            change = jnp.where(lane == 3 + c, drag * speeds[c][r * NB : (r + 1) * NB], change)
        arrived[pl.ds(r, NB, stride=CAP), :] = recv_b[pl.ds(r, NB, stride=CAP), :] * keep + change

    low_sel = ones(iota((NB, NB), 1).astype(F32) == column(low_partner[...].astype(F32)))
    high_sel = ones(iota((NB, NB), 1).astype(F32) == column(high_partner[...].astype(F32)))
    z_tiles = forward[pl.ds(1, NB * NQ, stride=2), :]
    z_tiles = (z_tiles[:64] + z_tiles[64:128]) + (z_tiles[128:192] + z_tiles[192:])
    below = pick_rows(low_sel, jnp.concatenate([recv_a[pl.ds(2, NB, stride=6), :], z_tiles], axis=1))
    above = pick_rows(high_sel, jnp.concatenate([recv_a[pl.ds(3, NB, stride=6), :], recv_a[pl.ds(4, NB, stride=6), :], z_tiles], axis=1))
    tiles = jnp.concatenate([below[:, :128], above[:, :128], above[:, 128:256], jnp.where(left, below[:, 128:], above[:, 256:])], axis=0)
    wide = pick_lanes(tiles, spread[...])
    mask = strip_mask()
    slots = ((0, 1), (3, 4), (6, 7), (2, 5))
    for g in range(4):
        for jt in range(8):
            block = wide[g * 64 + jt * 8 : g * 64 + jt * 8 + 8]
            for half in range(2):
                value = jnp.sum(jnp.where(mask, block[:, half * 512 : (half + 1) * 512], 0.0), axis=0, keepdims=True)
                ghosts[slots[g][half] : slots[g][half] + 1, jt * 512 : (jt + 1) * 512] = value

    lane = iota((LAYERS, 128), 1)
    layer = iota((LAYERS, 128), 0)
    fuel = jnp.where(q == 0, 1.0, 0.0)
    right_half = lane >= 64
    inside = (lane & 63) != 0

    def strip(n, carry):
        i = LAYERS - 1 - n
        here = pl.ds(pl.multiple_of(i * 128, 128), 128)
        back = pl.ds(pl.multiple_of(jnp.maximum(i - 1, 0) * 128, 128), 128)
        beyond_wall = (i > 0) | right_half

        def below_of(x, ghost):
            return jnp.where(layer == 0, ghost, pltpu.roll(x, 1, 0))

        def before_of(x, previous):
            return pltpu.roll(jnp.where(right_half, previous, x), 64, 1)

        z = z_sum[:, here]
        g0, g1, g2 = diffusion[0, :, here], diffusion[1, :, here], diffusion[2, :, here]
        gt = ghosts[7:8, here]
        h0 = 0.5 * (flow[0, :, here] + g0 * (z - below_of(z, ghosts[2:3, here])))
        ht = 0.5 * (ghosts[6:7, here] + gt * (ghosts[5:6, here] - z[LAYERS - 1 :]))
        h1 = 0.5 * (flow[1, :, here] + g1 * (z - before_of(z, z_sum[:, back])))
        h2 = 0.5 * (flow[2, :, here] + g2 * (z - pltpu.roll(z, 1, 1)))
        h1, g1 = jnp.where(beyond_wall, h1, 0.0), jnp.where(beyond_wall, g1, 0.0)
        h2, g2 = jnp.where(inside, h2, 0.0), jnp.where(inside, g2, 0.0)
        half_inv = STEP * inv_volume[:, here]
        src = source[pl.ds(pl.multiple_of(i * LAYERS, LAYERS), LAYERS), :]
        out = []
        for s in range(2):
            y = species[s, :, here]
            top = ghosts[3 + s : 4 + s, here]
            last = y[LAYERS - 1 :]
            y0 = below_of(y, ghosts[s : s + 1, here])
            y1 = before_of(y, species[s, :, back])
            y2 = pltpu.roll(y, 1, 1)
            f0 = h0 * (y + y0) - (g0 * d[s]) * (y - y0)
            ft = ht * (top + last) - (gt * d[s]) * (top - last)
            f1 = h1 * (y + y1) - (g1 * d[s]) * (y - y1)
            f2 = h2 * (y + y2) - (g2 * d[s]) * (y - y2)
            u0 = jnp.where(layer == LAYERS - 1, ft, pltpu.roll(f0, LAYERS - 1, 0))
            u1 = pltpu.roll(jnp.where(right_half, f1, carry[s]), 64, 1)
            u2 = pltpu.roll(f2, 127, 1)
            divergence = (u0 - f0) + ((u1 - f1) + (u2 - f2))
            delta = fuel if s == 0 else 0.0
            new_species[s, :, here] = y + half_inv * (src * (delta - y) - divergence)
            out.append(f1)
        return tuple(out)

    lax.fori_loop(0, LAYERS, strip, (jnp.zeros((LAYERS, 128), F32),) * 2)


def spec(space=pltpu.VMEM):
    return pl.BlockSpec(memory_space=space)


ANY = pl.BlockSpec(memory_space=pl.ANY)


def params(**kw):
    return pltpu.CompilerParams(vmem_limit_bytes=VMEM_LIMIT, **kw)


def shape(*dims):
    return jax.ShapeDtypeStruct(dims, F32)


def body(
    species, interface_normal_flow, face_diffusion, inv_volume, diffusivity, low_partner, high_partner,
    low_orient, high_orient, droplet_table, parcel_block, parcel_cell, parcel_live,
):
    pick, oriented, unoriented, spread = constants()
    first = pl.BlockSpec((1, 8, JK), lambda i: (0, 0, 0))
    whole = lambda *dims: pl.BlockSpec(dims, lambda i: (0,) * len(dims))
    msg_a, msg_b, z_part = pl.pallas_call(
        prep_kernel,
        grid=(1,),
        out_shape=(shape(384, 128), shape(384, 128), shape(LAYERS, JK)),
        in_specs=[
            pl.BlockSpec(memory_space=pltpu.SMEM), whole(2, LAYERS, JK), first, first,
            *[whole(1, 64)] * 4, whole(256, 128), *[whole(1, 256)] * 3,
            whole(512, 64), whole(64, 1024), whole(64, 1024),
        ],
        out_specs=(whole(384, 128), whole(384, 128), whole(LAYERS, JK)),
        compiler_params=params(),
        name="prep",
    )(
        diffusivity, species, interface_normal_flow, face_diffusion, low_partner, high_partner, low_orient, high_orient,
        droplet_table, parcel_block.reshape(1, -1), parcel_cell.reshape(1, -1), parcel_live.reshape(1, -1),
        pick, oriented, unoriented,
    )
    dma = pltpu.SemaphoreType.DMA
    recv_a, recv_b, z_sum, forward = pl.pallas_call(
        exchange_kernel,
        out_shape=(shape(NB, 3, 2, 128), shape(NB, 3, 2, 128), shape(NQ, 8, JK), shape(NQ, NB, 2, 128)),
        in_specs=[ANY] * 3,
        out_specs=(ANY,) * 4,
        scratch_shapes=[
            pltpu.VMEM((3, 8, JK), F32), pltpu.VMEM((8, JK), F32), pltpu.VMEM((8, JK), F32),
            dma((3, 3)), dma((3, 3)), dma((2,)), dma((2,)), dma((5,)),
        ],
        compiler_params=params(collective_id=0, has_side_effects=True),
        name="exchange",
    )(msg_a.reshape(NB, 3, 2, 128), msg_b.reshape(NB, 3, 2, 128), z_part.reshape(NQ, 8, JK))
    forward = forward.reshape(NQ * NB * 2, 128)
    mine = pl.pallas_call(
        fuel_kernel,
        grid=(1,),
        out_shape=shape(8, NB * NQ),
        in_specs=[whole(NQ * NB * 2, 128), whole(1, LAYERS, JK)],
        out_specs=whole(8, NB * NQ),
        compiler_params=params(),
        name="fuel",
    )(forward, species)
    found = pl.pallas_call(
        share_kernel,
        out_shape=shape(8, NB * NQ),
        in_specs=[ANY],
        out_specs=ANY,
        scratch_shapes=[dma((3,)), dma, dma],
        compiler_params=params(collective_id=1, has_side_effects=True),
        name="share",
    )(mine)
    new_species, arrived = pl.pallas_call(
        final_kernel,
        out_shape=(shape(2, LAYERS, JK), shape(384, 128)),
        in_specs=[pl.BlockSpec(memory_space=pltpu.SMEM)] + [spec()] * 12,
        out_specs=(spec(), spec()),
        scratch_shapes=[pltpu.VMEM((8, JK), F32), pltpu.VMEM((1024, 128), F32), pltpu.VMEM((256, 128), F32)],
        compiler_params=params(),
        name="final",
    )(
        diffusivity, species, interface_normal_flow, face_diffusion, inv_volume, z_sum.reshape(LAYERS, JK),
        low_partner, high_partner, recv_a.reshape(384, 128), recv_b.reshape(384, 128), forward, found, spread,
    )
    return new_species, arrived


def solution(mesh):
    placed = (
        P("sp", "blk", None), P(None, "blk", None), P(None, "blk", None), P("blk", None), P("sp"),
        P("blk", None), P("blk", None), P("blk", None), P("blk", None),
        P(("blk", "sp"), None), P(("blk", "sp"), None), P(("blk", "sp")), P(("blk", "sp")),
    )
    return jax.shard_map(
        body, mesh=mesh, in_specs=placed, out_specs=(P("sp", "blk", None), P(("blk", "sp"), None)), check_vma=False,
    )
```

time: 279 us -> 66.1 us (0.24); the launches traced: 275 us -> 65.7 us
  local copies, waits for them, and re-layouts: 98.2 us -> 13 us
  other arithmetic: 53.4 us -> 0 us
  Pallas kernels: 0 us -> 52 us
  waiting for transfers between devices: 49.9 us -> 0 us
  starting transfers between devices: 42.9 us -> 0 us
  blocking collectives: 15.5 us -> 0 us
  between operations: 15.1 us -> 0.73 us
    pallas_call x0 -> x5, Pallas kernels: none -> 52 us  [the longest x1 29 us: body(): pl.pallas_call(exchange_kernel, out_shape=(shape(NB, 3, 2, 128), shape(NB...]
    all_to_all x5 -> x0, starting transfers between devices: 42.8 us -> none  [the longest x1 12.1 us: body(): lax.all_to_all(send_cells, 'blk', split_axis=0, concat_axis=0, tiled=True)]
    psum x2 -> x0, waiting for transfers between devices: 27.7 us -> none  [the longest x1 27.7 us: body(): lax.psum((partial_terms[0], partial_terms[1], partial_terms[2], partial_t...]
    unnamed x97 -> x38, local copies, waits for them, and re-layouts: 37.8 us -> 13 us
    gather x6 -> x0, local copies, waits for them, and re-layouts: 23 us -> none  [the longest x1 11 us: body(): evaporate_component = fuel_field[landing_grid_points]]
    all_to_all x5 -> x0, waiting for transfers between devices: 22.2 us -> none  [the longest x1 8.1 us: body(): lax.all_to_all(send_flags, 'blk', split_axis=0, concat_axis=0, tiled=True)]
    psum x1 -> x0, blocking collectives: 15.5 us -> none  [body(): lax.psum((partial_terms[0], partial_terms[1], partial_terms[2], partial_t...]
    mul x10 -> x0, other arithmetic: 11.4 us -> none  [the longest x2 5.18 us: face_flux(): diffusion * (scaled * difference - middle * weight)]
  transfers between devices with their start and end apart: 7 -> 0, of which waited for: 4 -> 0; matrix products, arithmetic and copies ran while one was open for 40% -> 0% of each run, Pallas kernels for 0% -> 0%
where the time goes in v1:
time: 66.1 us; the launch traced here: 65.7 us
  Pallas kernels  52 us (79%)
  local copies, waits for them, and re-layouts  13 us (20%)
  between operations  0.73 us (1%)
    pallas_call x1, Pallas kernels, body(): pl.pallas_call(exchange_kernel, out_shape=(shape(NB, 3, 2, 128), shape(NB...  29 us
    unnamed x38, local copies, waits for them, and re-layouts  13 us
    pallas_call x1, Pallas kernels, body(): pl.pallas_call(final_kernel, out_shape=(shape(2, LAYERS, JK), shape(384,...  12.2 us
    pallas_call x1, Pallas kernels, body(): pl.pallas_call(share_kernel, out_shape=shape(8, NB * NQ), in_specs=[ANY],...  6.03 us
    pallas_call x1, Pallas kernels, body(): pl.pallas_call(prep_kernel, grid=(1,), out_shape=(shape(384, 128), shape(...  2.75 us
    pallas_call x1, Pallas kernels, body(): pl.pallas_call(fuel_kernel, grid=(1,), out_shape=shape(8, NB * NQ), in_sp...  2 us

profile of v1, /device:TPU:2, one launch (start us, length us, event | category | flops | bytes accessed | tf_op | source)
XLA Modules:
  0.0 65.7 jit_solution(5852193817697996172)
XLA Ops:
  0.6 0.0 copy-start
  0.6 1.2 %copy-done = f32[2,32,4096]{2,1,0:T(8,128)S(1)} copy-done((f32[2,32,4096]{2,1,0:T(8,128)S(1)}, f32[2,32,4096]{2,1,0:T(8,128)}, u32[]{:S(2)}) %copy-start) | copy-done | bytes 1048600
  1.9 0.0 copy-start.2
  1.9 1.4 %copy-done.2 = f32[3,32,4096]{2,1,0:T(8,128)S(1)} copy-done((f32[3,32,4096]{2,1,0:T(8,128)S(1)}, f32[3,32,4096]{2,1,0:T(8,128)}, u32[]{:S(2)}) %copy-start.2) | copy-done | bytes 1572888
  3.3 0.0 copy-start.4
  3.3 1.4 %copy-done.4 = f32[3,32,4096]{2,1,0:T(8,128)S(1)} copy-done((f32[3,32,4096]{2,1,0:T(8,128)S(1)}, f32[3,32,4096]{2,1,0:T(8,128)}, u32[]{:S(2)}) %copy-start.4) | copy-done | bytes 1572888
  4.7 0.0 copy-start.7
  4.7 0.9 %copy-done.7 = f32[256,128]{1,0:T(8,128)S(1)} copy-done((f32[256,128]{1,0:T(8,128)S(1)}, f32[256,128]{1,0:T(8,128)}, u32[]{:S(2)}) %copy-start.7) | copy-done | bytes 131096
  5.6 0.0 copy-start.8
  5.6 0.9 %copy-done.8 = bf16[64,1024]{1,0:T(8,128)(2,1)S(1)} copy-done((bf16[64,1024]{1,0:T(8,128)(2,1)S(1)}, bf16[64,1024]{1,0:T(8,128)(2,1)}, u32[]{:S(2)}) %copy-start.8) | copy-done | bytes 131096
  6.5 0.0 copy-start.9
  6.5 0.9 %copy-done.9 = bf16[64,1024]{1,0:T(8,128)(2,1)S(1)} copy-done((bf16[64,1024]{1,0:T(8,128)(2,1)S(1)}, bf16[64,1024]{1,0:T(8,128)(2,1)}, u32[]{:S(2)}) %copy-start.9) | copy-done | bytes 131096
  7.4 0.0 copy-start.10
  7.4 0.9 %copy-done.10 = bf16[512,64]{1,0:T(8,128)(2,1)S(1)} copy-done((bf16[512,64]{1,0:T(8,128)(2,1)S(1)}, bf16[512,64]{1,0:T(8,128)(2,1)}, u32[]{:S(2)}) %copy-start.10) | copy-done | bytes 65560
  8.3 0.0 copy-start.11
  8.3 0.7 copy-done.11
  9.0 0.0 copy-start.12
  9.0 0.7 copy-done.12
  9.6 0.0 copy-start.13
  9.6 0.7 copy-done.13
  10.3 0.0 copy-start.14
  10.3 0.7 %copy-done.14 = s32[256,1]{0,1:T(1,128)S(1)} copy-done((s32[256,1]{0,1:T(1,128)S(1)}, s32[256,1]{0,1:T(1,128)}, u32[]{:S(2)}) %copy-start.14) | copy-done | bytes 1048
  10.9 0.0 copy-start.15
  10.9 0.7 %copy-done.15 = s32[256]{0:T(256)S(1)} copy-done((s32[256]{0:T(256)S(1)}, s32[256]{0:T(256)}, u32[]{:S(2)}) %copy-start.15) | copy-done | bytes 1048
  11.6 0.0 copy-start.16
  11.6 0.7 %copy-done.16 = s32[256]{0:T(256)S(1)} copy-done((s32[256]{0:T(256)S(1)}, s32[256]{0:T(256)}, u32[]{:S(2)}) %copy-start.16) | copy-done | bytes 1048
  12.3 0.0 copy-start.17
  12.3 0.7 copy-done.17
  13.0 0.0 copy-start.18
  13.0 0.7 copy-done.18
  13.6 0.0 copy-start.1
  13.6 0.0 copy-start.6
  13.6 2.7 %prep.1 = (f32[384,128]{1,0:T(8,128)S(1)}, f32[384,128]{1,0:T(8,128)S(1)}, f32[32,4096]{1,0:T(8,128)S(1)}) custom-call(f32[2]{0:T(128)S(1)} %copy-done.11, f32[2,32,4096]{2,1,0:T(8,128)S(1)} %copy-done, f32[3,32,4096]{2,1,0:T(8,128)S(1)} %copy-done.2, f32[3,32,4096]{2,1,0:T(8,128)S(1)} %copy-done.4, s32[1,64]{1,0:T(1,128)S(1)} %copy-done.12, ...), custom_call_target="tpu_custom_call" | custom-call | tf_op jit(solution)/shard_map/prep/pallas_call | solution.py:415
  16.4 0.0 copy-start.3
  16.4 0.0 copy-start.5
  16.4 29.0 %exchange.1 = (f32[64,3,2,128]{3,2,1,0:T(2,128)S(1)}, f32[64,3,2,128]{3,2,1,0:T(2,128)S(1)}, f32[4,8,4096]{2,1,0:T(8,128)S(1)}, f32[4,64,2,128]{3,2,1,0:T(2,128)S(1)}) custom-call(f32[64,3,2,128]{3,2,1,0:T(2,128)S(1)} %bitcast.16, f32[64,3,2,128]{3,2,1,0:T(2,128)S(1)} %bitcast.17, f32[4,8,4096]{2,1,0:T(8,128)S(1)} %bitcast.12), custom_call_target="tpu_custom_call" | custom-call | tf_op jit(solution)/shard_map/exchange/pallas_call | solution.py:433
  45.4 0.0 copy-done.1
  45.5 2.0 %fuel.2.mine = f32[8,256]{1,0:T(8,128)S(1)} custom-call(f32[512,128]{1,0:T(8,128)S(1)} %bitcast.10, f32[2,32,4096]{2,1,0:T(8,128)S(1)} %copy-done.1), custom_call_target="tpu_custom_call" | custom-call | tf_op jit(solution)/shard_map/fuel/pallas_call | solution.py:446
  47.5 6.0 %share.1.found = f32[8,256]{1,0:T(8,128)S(1)} custom-call(f32[8,256]{1,0:T(8,128)S(1)} %fuel.2.mine), custom_call_target="tpu_custom_call" | custom-call | tf_op jit(solution)/shard_map/share/pallas_call | solution.py:455
  53.5 0.0 copy-done.6
  53.5 0.0 copy-done.3
  53.5 0.0 copy-done.5
  53.5 12.2 %final.1 = (f32[2,32,4096]{2,1,0:T(8,128)}, f32[384,128]{1,0:T(8,128)}) custom-call(f32[2]{0:T(128)S(1)} %copy-done.11, f32[2,32,4096]{2,1,0:T(8,128)S(1)} %copy-done.1, f32[3,32,4096]{2,1,0:T(8,128)S(1)} %copy-done.3, f32[3,32,4096]{2,1,0:T(8,128)S(1)} %copy-done.4, f32[32,4096]{1,0:T(8,128)S(1)} %copy-done.5, f32[32,4096]{1,0:T(8,128)S(1)} %bitcast.13, ...), custom_call_target="tpu_custom_call" | custom-call | tf_op jit(solution)/shard_map/final/pallas_call | solution.py:464
Async XLA Ops:
  0.6 1.2 %copy-start = (f32[2,32,4096]{2,1,0:T(8,128)S(1)}, f32[2,32,4096]{2,1,0:T(8,128)}, u32[]{:S(2)}) copy-start(f32[2,32,4096]{2,1,0:T(8,128)} %species.3) | copy-start | bytes 3145732
  1.9 1.4 %copy-start.2 = (f32[3,32,4096]{2,1,0:T(8,128)S(1)}, f32[3,32,4096]{2,1,0:T(8,128)}, u32[]{:S(2)}) copy-start(f32[3,32,4096]{2,1,0:T(8,128)} %flow.3) | copy-start | bytes 4718596
  3.3 1.4 %copy-start.4 = (f32[3,32,4096]{2,1,0:T(8,128)S(1)}, f32[3,32,4096]{2,1,0:T(8,128)}, u32[]{:S(2)}) copy-start(f32[3,32,4096]{2,1,0:T(8,128)} %diffusion.3) | copy-start | bytes 4718596
  4.7 0.9 %copy-start.7 = (f32[256,128]{1,0:T(8,128)S(1)}, f32[256,128]{1,0:T(8,128)}, u32[]{:S(2)}) copy-start(f32[256,128]{1,0:T(8,128)} %table.1) | copy-start | bytes 393220
  5.6 0.9 %copy-start.8 = (bf16[64,1024]{1,0:T(8,128)(2,1)S(1)}, bf16[64,1024]{1,0:T(8,128)(2,1)}, u32[]{:S(2)}) copy-start(bf16[64,1024]{1,0:T(8,128)(2,1)} %constant.10.clone.unoriented) | copy-start | bytes 393220
  6.5 0.9 %copy-start.9 = (bf16[64,1024]{1,0:T(8,128)(2,1)S(1)}, bf16[64,1024]{1,0:T(8,128)(2,1)}, u32[]{:S(2)}) copy-start(bf16[64,1024]{1,0:T(8,128)(2,1)} %constant.9.clone.oriented) | copy-start | bytes 393220
  7.4 0.9 %copy-start.10 = (bf16[512,64]{1,0:T(8,128)(2,1)S(1)}, bf16[512,64]{1,0:T(8,128)(2,1)}, u32[]{:S(2)}) copy-start(bf16[512,64]{1,0:T(8,128)(2,1)} %constant.8.clone.pick) | copy-start | bytes 196612
  8.3 0.7 copy-start.11
  9.0 0.7 copy-start.12
  9.6 0.7 copy-start.13
  10.3 0.7 %copy-start.14 = (s32[256,1]{0,1:T(1,128)S(1)}, s32[256,1]{0,1:T(1,128)}, u32[]{:S(2)}) copy-start(s32[256,1]{0,1:T(1,128)} %param.27) | copy-start | bytes 3076
  10.9 0.7 %copy-start.15 = (s32[256]{0:T(256)S(1)}, s32[256]{0:T(256)}, u32[]{:S(2)}) copy-start(s32[256]{0:T(256)} %param.28) | copy-start | bytes 3076
  11.6 0.7 %copy-start.16 = (s32[256]{0:T(256)S(1)}, s32[256]{0:T(256)}, u32[]{:S(2)}) copy-start(s32[256]{0:T(256)} %param.29) | copy-start | bytes 3076
  12.3 0.7 copy-start.17
  13.0 0.7 copy-start.18
  13.6 31.8 %copy-start.1 = (f32[2,32,4096]{2,1,0:T(8,128)S(1)}, f32[2,32,4096]{2,1,0:T(8,128)}, u32[]{:S(2)}) copy-start(f32[2,32,4096]{2,1,0:T(8,128)} %species.3) | copy-start | bytes 3145732
  13.6 39.9 %copy-start.6 = (bf16[128,1024]{1,0:T(8,128)(2,1)S(1)}, bf16[128,1024]{1,0:T(8,128)(2,1)}, u32[]{:S(2)}) copy-start(bf16[128,1024]{1,0:T(8,128)(2,1)} %constant.11.clone.spread) | copy-start | bytes 786436
  16.4 37.1 %copy-start.3 = (f32[3,32,4096]{2,1,0:T(8,128)S(1)}, f32[3,32,4096]{2,1,0:T(8,128)}, u32[]{:S(2)}) copy-start(f32[3,32,4096]{2,1,0:T(8,128)} %flow.3) | copy-start | bytes 4718596
  16.4 37.1 %copy-start.5 = (f32[32,4096]{1,0:T(8,128)S(1)}, f32[32,4096]{1,0:T(8,128)}, u32[]{:S(2)}) copy-start(f32[32,4096]{1,0:T(8,128)} %inv_volume.1) | copy-start | bytes 1572868

commit v2 on v1

v2 whole, which is shorter than its diff:
```python
import functools
import jax
import jax.numpy as jnp
import numpy as np
from jax import lax
from jax.experimental import pallas as pl
from jax.experimental.pallas import tpu as pltpu
from jax.sharding import PartitionSpec as P

NB = 64
NQ = 4
CAP = 6
ROWS = 8
CHUNKS = 2
LAYERS = 32
JK = 4096
MESH = pl.DeviceIdType.MESH
F32 = jnp.float32
BF16 = jnp.bfloat16
STEP = 0.5
DRAG = 0.3
VMEM_LIMIT = 36 * 1024 * 1024


def constants():
    lane = np.arange(512)
    cell = np.arange(64)
    pick = (lane[:, None] // 64 == cell[None, :] // 8) & (lane[:, None] % 8 == cell[None, :] % 8)
    r, c = cell // 8, cell % 8
    oriented, unoriented = [], []
    for code in range(8):
        f_row = (lambda v: 7 - v) if code & 1 else (lambda v: v)
        f_col = (lambda v: 7 - v) if code & 2 else (lambda v: v)
        r2, c2 = f_row(r), f_col(c)
        source = c2 * 8 + r2 if code & 4 else r2 * 8 + c2
        oriented += [cell[:, None] == source[None, :]] * 2
        source = f_row(c) * 8 + f_col(r) if code & 4 else f_row(r) * 8 + f_col(c)
        unoriented += [cell[:, None] == source[None, :]] * 2
    spread = np.zeros((128, 1024), bool)
    spread[:64, :512] = pick.T
    spread[64:, 512:] = pick.T
    asb = lambda m: jnp.asarray(m.astype(np.float32), BF16)
    return asb(pick), asb(np.concatenate(oriented, 1)), asb(np.concatenate(unoriented, 1)), asb(spread)


def pieces(x):
    hi = x.astype(BF16)
    rest = x - hi.astype(F32)
    mid = rest.astype(BF16)
    low = (rest - mid.astype(F32)).astype(BF16)
    return hi, mid, low


def mm(a, b):
    return lax.dot_general(a, b, (((1,), (0,)), ((), ())), preferred_element_type=F32)


def pick_rows(onehot, x):
    hi, mid, low = pieces(x)
    return (mm(onehot, hi) + mm(onehot, mid)) + mm(onehot, low)


def pick_lanes(x, onehot):
    hi, mid, low = pieces(x)
    return (mm(hi, onehot) + mm(mid, onehot)) + mm(low, onehot)


def iota(shape, axis):
    return lax.broadcasted_iota(jnp.int32, shape, axis)


def ones(mask):
    return jnp.where(mask, 1.0, 0.0).astype(BF16)


def column(row):
    n = row.shape[1]
    return jnp.sum(jnp.where(iota((n, n), 0) == iota((n, n), 1), row, 0.0), axis=1, keepdims=True)


def strip_mask():
    lane = iota((8, 512), 1)
    return (lane % 64) // 8 == iota((8, 512), 0)


def stack_field(ref_slice):
    return jnp.concatenate([ref_slice[:, i * 128 : (i + 1) * 128] for i in range(LAYERS)], axis=0)


def lookup(cells, field3):
    return lookups(cells, [field3])[0]


def lookups(cells, fields):
    n = cells.shape[0]
    whole = cells.astype(jnp.int32)
    row = ((whole & 4095) >> 7) * LAYERS + (whole >> 12)
    hot = ones(iota((n, 1024), 1) == row)
    here = iota((n, 128), 1) == (whole & 127)
    out = []
    for field3 in fields:
        got = mm(hot, field3)
        got = (got[:, :128] + got[:, 128:256]) + got[:, 256:]
        out.append(jnp.sum(jnp.where(here, got, 0.0), axis=1, keepdims=True))
    return out


def build_messages(
    d0, d1, species, flow, diffusion, low_partner, high_partner, low_orient, high_orient,
    table, block, cell, live, pick, oriented, unoriented, msg_a, msg_b,
):
    n = table.shape[0]
    alive = live[...] == 1
    target = block[...].astype(F32)
    key = jnp.where(alive, target, -1.0)
    key_col = column(key)
    same = key_col == key
    first, second = iota((n, n), 0), iota((n, n), 1)
    rank = jnp.sum(jnp.where(same & (first < second), 1.0, 0.0), axis=0, keepdims=True)
    rank_col = jnp.sum(jnp.where(same & (second < first), 1.0, 0.0), axis=1, keepdims=True)
    slot = jnp.where(alive, target * ROWS + rank, -1.0)
    rows = table[...]
    place = ones(iota((NB * ROWS, n), 0).astype(F32) == slot)
    msg_b[...] = pick_rows(place, rows)

    lane = iota((n, 128), 1)
    cell_col = column(cell[...].astype(F32))
    boil = jnp.maximum(rows, 0.0) + jnp.log1p(jnp.exp(-jnp.abs(rows)))
    sig = 1.0 / (1.0 + jnp.exp(-rows))
    kind = lane & 7
    meta = jnp.where(kind == 0, cell_col, jnp.where(kind == 1, boil[:, 1:2], jnp.where(kind == 2, sig[:, 2:3], jnp.where(kind == 3, 1.0, 0.0))))
    meta = jnp.where((lane >> 3).astype(F32) == rank_col, meta, 0.0)

    mask = strip_mask()
    faces = [
        species[0, LAYERS - 1 : LAYERS, :], species[1, LAYERS - 1 : LAYERS, :],
        species[0, 0:1, :], species[1, 0:1, :], flow[0, 0:1, :], diffusion[0:1, :],
    ]
    strips = []
    for face in faces:
        for jt in range(8):
            strips.append(jnp.where(mask, face[:, jt * 512 : (jt + 1) * 512], 0.0))
    tiles = pick_lanes(jnp.concatenate(strips, axis=0), pick[...])
    turned = pick_lanes(tiles[:128], oriented[...])
    unturned = pick_lanes(tiles[128:], unoriented[...])
    high_code = column(high_orient[...].astype(F32))
    low_code = column(low_orient[...].astype(F32))

    def choose(x, code):
        out = x[:, :128]
        for o in range(1, 8):
            out = jnp.where(code == o, x[:, o * 128 : (o + 1) * 128], out)
        return out

    up0, up1 = (choose(turned[k * 64 : (k + 1) * 64], high_code) for k in range(2))
    lo0, lo1, fl, df = (choose(unturned[k * 64 : (k + 1) * 64], low_code) for k in range(4))
    left = iota((NB, 128), 1) < 64
    values = jnp.concatenate(
        [
            meta,
            jnp.where(left, up0, up1),
            jnp.where(left, lo0, lo1),
            jnp.where(left, fl, df),
            jnp.where(left, d0 * up0 + d1 * up1, 0.0),
            jnp.where(left, 0.0, d0 * lo0 + d1 * lo1),
        ],
        axis=0,
    )
    hp, lp = high_partner[...].astype(F32) * ROWS, low_partner[...].astype(F32) * ROWS
    keys = jnp.concatenate([jnp.where(alive, target * ROWS, -1.0), hp + 2.0, lp + 3.0, lp + 4.0, hp + 1.0, lp + 1.0], axis=1)
    where_to = ones(iota((NB * ROWS, keys.shape[1]), 0).astype(F32) == keys)
    msg_a[...] = pick_rows(where_to, values)


def exchange_kernel(
    dif_in, species_in, flow_in, diffusion_in, lp_in, hp_in, lo_in, ho_in, table_in, block_in, cell_in, live_in,
    pick_in, oriented_in, unoriented_in, spread_in,
    z_sum, source, ghosts, parcels, change,
    dif, species, flow, diffusion, lp, hp, lo, ho, table, block, cell, live, pick, oriented, unoriented, spread,
    msg_a, msg_b, recv_a, forward, z_part, z_got, z_mine, fuel_mine, fuel, hot,
    load_sems, sems, recv_sems, wide_send, wide_recv, local_sems, fuel_send, fuel_recv,
):
    b, q = lax.axis_index("blk"), lax.axis_index("sp")
    loads = [
        pltpu.make_async_copy(src, dst, load_sems.at[k])
        for k, (src, dst) in enumerate(
            (
                (dif_in, dif), (species_in, species), (flow_in, flow), (diffusion_in.at[0, pl.ds(0, 8)], diffusion),
                (lp_in, lp), (hp_in, hp), (lo_in, lo), (ho_in, ho), (table_in, table), (block_in, block),
                (cell_in, cell), (live_in, live), (pick_in, pick), (oriented_in, oriented), (unoriented_in, unoriented),
                (spread_in, spread),
            )
        )
    ]
    for load in loads:
        load.start()
    barrier = pltpu.get_barrier_semaphore()

    def greet(i, carry):
        pl.semaphore_signal(barrier, inc=1, device_id=(lax.rem(b + i, NB), q), device_id_type=MESH)
        return carry

    for d in range(1, NQ):
        pl.semaphore_signal(barrier, inc=1, device_id=(b, lax.rem(q + d, NQ)), device_id_type=MESH)
    lax.fori_loop(1, NB, greet, 0)
    for load in loads:
        load.wait()

    d0, d1 = dif[0], dif[1]
    for k in range(NQ):
        z_part[k] = d0 * species[0, k * 8 : (k + 1) * 8] + d1 * species[1, k * 8 : (k + 1) * 8]
    build_messages(
        d0, d1, species, flow, diffusion, lp, hp, lo, ho, table, block, cell, live, pick, oriented, unoriented,
        msg_a.reshape(NB * ROWS, 128), msg_b.reshape(NB * ROWS, 128),
    )
    pl.semaphore_wait(barrier, NB + NQ - 2)

    def sp_copy(src, dst, k, d):
        return pltpu.make_async_remote_copy(
            src_ref=src, dst_ref=dst, send_sem=sems.at[k, d - 1], recv_sem=recv_sems.at[k, d - 1],
            device_id=(b, lax.rem(q + d, NQ)), device_id_type=MESH,
        )

    wide = JK // CHUNKS
    part = [pl.ds(c * wide, wide) for c in range(CHUNKS)]
    scatter = [
        [sp_copy(z_part.at[lax.rem(q + d, NQ), :, part[c]], z_got.at[d - 1, :, part[c]], c, d) for d in (2, 1, 3)]
        for c in range(CHUNKS)
    ]
    for copies in scatter:
        for copy in copies:
            copy.start()

    rows_a, rows_b = pl.ds(0, 5), pl.ds(0, CAP)
    keep_a = pltpu.make_async_copy(msg_a.at[b, rows_a], recv_a.at[b, rows_a], local_sems.at[0])
    keep_b = pltpu.make_async_copy(msg_b.at[b, rows_b], parcels.at[b, rows_b], local_sems.at[1])
    keep_a.start()
    keep_b.start()

    def send(msg, recv, rows, k, start, stop):
        def step(i, carry):
            to = lax.rem(b + i, NB)
            pltpu.make_async_remote_copy(
                src_ref=msg.at[to, rows], dst_ref=recv.at[b, rows], send_sem=wide_send.at[k], recv_sem=wide_recv.at[k],
                device_id=(to, q), device_id_type=MESH,
            ).start()
            return carry

        lax.fori_loop(start, stop, step, 0)

    send(msg_a, recv_a, rows_a, 0, 1, NB)
    gather = []
    for c in range(CHUNKS):
        for copy in scatter[c]:
            copy.wait_recv()
        z_mine[:, part[c]] = (z_part[q, :, part[c]] + z_got[0, :, part[c]]) + (z_got[1, :, part[c]] + z_got[2, :, part[c]])
        copies = [sp_copy(z_mine.at[:, part[c]], z_sum.at[q, :, part[c]], CHUNKS + c, d) for d in (2, 1, 3)]
        for copy in copies:
            copy.start()
        gather += copies
    z_sum[q] = z_mine[...]

    most = pl.ds(0, NB - 1)
    keep_a.wait()
    pltpu.make_async_copy(recv_a.at[most, rows_a], recv_a.at[most, rows_a], wide_recv.at[0]).wait()
    two = pl.ds(0, 2)
    onward = [sp_copy(recv_a.at[:, two], forward.at[q, :, two], 2 * CHUNKS, d) for d in (2, 1, 3)]
    for copy in onward:
        copy.start()
    keep_f = pltpu.make_async_copy(recv_a.at[:, two], forward.at[q, :, two], local_sems.at[2])
    keep_f.start()
    send(msg_b, parcels, rows_b, 1, 1, NB)

    got = recv_a.reshape(NB * ROWS, 128)
    seen = forward.reshape(NQ * NB * ROWS, 128)
    own = got[pl.ds(0, NB, stride=ROWS), :]
    own_cells = jnp.concatenate([own[:, 8 * r : 8 * r + 1] for r in range(CAP)], axis=0)

    keep_f.wait()
    for copy in onward:
        copy.wait_recv()
    meta = seen[pl.ds(0, NB * NQ, stride=ROWS), :]

    @pl.when(q == 0)
    def _():
        field3 = jnp.concatenate(pieces(stack_field(species[0])), axis=1)
        lane = iota((NB * NQ, 128), 1)
        found = jnp.zeros((NB * NQ, 128), F32)
        for r in range(CAP):
            found = jnp.where(lane == r, lookup(meta[:, 8 * r : 8 * r + 1], field3), found)
        fuel_mine[...] = jnp.transpose(found)[:8]
        copies = [
            pltpu.make_async_remote_copy(
                src_ref=fuel_mine, dst_ref=fuel, send_sem=fuel_send.at[d - 1], recv_sem=fuel_recv, device_id=(b, d), device_id_type=MESH
            )
            for d in (2, 1, 3)
        ]
        for copy in copies:
            copy.start()
        keep = pltpu.make_async_copy(fuel_mine, fuel, local_sems.at[3])
        keep.start()
        keep.wait()
        for copy in copies:
            copy.wait_send()

    meta_t = jnp.transpose(meta)
    cells = jnp.concatenate([meta_t[8 * r : 8 * r + 1, :] for r in range(CAP)], axis=1).astype(jnp.int32)
    row = ((cells & 4095) >> 7) * LAYERS + (cells >> 12)
    for m in range(4):
        hot[m * 256 : (m + 1) * 256, :] = ones(iota((256, NB * NQ * CAP), 0) + m * 256 == row)
    speeds = lookups(own_cells, [jnp.concatenate(pieces(stack_field(flow[k])), axis=1) for k in range(3)])

    low_sel = ones(iota((NB, NB), 1).astype(F32) == column(lp[...].astype(F32)))
    high_sel = ones(iota((NB, NB), 1).astype(F32) == column(hp[...].astype(F32)))
    z_tiles = seen[pl.ds(1, NB * NQ, stride=ROWS), :]
    z_tiles = (z_tiles[:64] + z_tiles[64:128]) + (z_tiles[128:192] + z_tiles[192:])
    left = iota((NB, 128), 1) < 64
    below = pick_rows(low_sel, jnp.concatenate([got[pl.ds(2, NB, stride=ROWS), :], z_tiles], axis=1))
    above = pick_rows(high_sel, jnp.concatenate([got[pl.ds(3, NB, stride=ROWS), :], got[pl.ds(4, NB, stride=ROWS), :], z_tiles], axis=1))
    tiles = jnp.concatenate([below[:, :128], above[:, :128], above[:, 128:256], jnp.where(left, below[:, 128:], above[:, 256:])], axis=0)
    spread_tiles = pick_lanes(tiles, spread[...])
    mask = strip_mask()
    slots = ((0, 1), (3, 4), (6, 7), (2, 5))
    for g in range(4):
        for jt in range(8):
            strip = spread_tiles[g * 64 + jt * 8 : g * 64 + jt * 8 + 8]
            for half in range(2):
                value = jnp.sum(jnp.where(mask, strip[:, half * 512 : (half + 1) * 512], 0.0), axis=0, keepdims=True)
                ghosts[slots[g][half] : slots[g][half] + 1, jt * 512 : (jt + 1) * 512] = value

    @pl.when(q != 0)
    def _():
        pltpu.make_async_copy(fuel_mine, fuel, fuel_recv).wait()

    found_col = jnp.transpose(jnp.concatenate([fuel[...], jnp.zeros((120, NB * NQ), F32)], axis=0))
    lane = iota((NB * NQ, 128), 1)
    mass = []
    for r in range(CAP):
        k = 8 * r
        gone = meta[:, k + 1 : k + 2] * (meta[:, k + 2 : k + 3] - found_col[:, r : r + 1])
        at = meta[:, k : k + 1].astype(jnp.int32) & 127
        mass.append(jnp.concatenate(pieces(jnp.where(lane == at, gone, 0.0)), axis=1))
    part3 = mm(hot[...], jnp.concatenate(mass, axis=0))
    source[...] = (part3[:, :128] + part3[:, 128:256]) + part3[:, 256:]

    group = iota((NB, NB * NQ), 1) - q * NB == iota((NB, NB * NQ), 0)
    own_fuel = pick_rows(ones(group), found_col)
    lane = iota((NB, 128), 1)
    for r in range(CAP):
        k = 8 * r
        gone = own[:, k + 1 : k + 2] * (own[:, k + 2 : k + 3] - own_fuel[:, r : r + 1])
        drag = DRAG * own[:, k + 3 : k + 4]
        moved = jnp.where(lane == 0, -gone, 0.0)
        for c in range(3):
            moved = jnp.where(lane == 3 + c, drag * speeds[c][r * NB : (r + 1) * NB], moved)
        change[pl.ds(r, NB, stride=CAP), :] = moved

    pltpu.make_async_copy(msg_a.at[most, rows_a], msg_a.at[most, rows_a], wide_send.at[0]).wait()
    pltpu.make_async_copy(msg_b.at[most, rows_b], msg_b.at[most, rows_b], wide_send.at[1]).wait()
    for copies in scatter:
        for copy in copies:
            copy.wait_send()
    for copy in onward:
        copy.wait_send()
    for copy in gather:
        copy.wait()
    keep_b.wait()
    pltpu.make_async_copy(parcels.at[most, rows_b], parcels.at[most, rows_b], wide_recv.at[1]).wait()


def final_kernel(
    dif, species, flow, diffusion, inv_volume, z_sum, source, ghosts, parcels, change, new_species, arrived, out, out_sems,
):
    q = lax.axis_index("sp")
    d = (dif[0], dif[1])
    lane = iota((NB, 128), 1)
    keep = jnp.where((lane >= 3) & (lane <= 5), 1.0 - DRAG, 1.0)
    for r in range(CAP):
        arrived[pl.ds(r, NB, stride=CAP), :] = parcels[pl.ds(r, NB, stride=ROWS), :] * keep + change[pl.ds(r, NB, stride=CAP), :]

    lane = iota((LAYERS, 128), 1)
    layer = iota((LAYERS, 128), 0)
    fuel = jnp.where(q == 0, 1.0, 0.0)
    right_half = lane >= 64
    inside = (lane & 63) != 0

    def strip(n, carry):
        i = LAYERS - 1 - n
        here = pl.ds(pl.multiple_of(i * 128, 128), 128)
        back = pl.ds(pl.multiple_of(jnp.maximum(i - 1, 0) * 128, 128), 128)
        beyond_wall = (i > 0) | right_half

        def below_of(x, ghost):
            return jnp.where(layer == 0, ghost, pltpu.roll(x, 1, 0))

        def before_of(x, previous):
            return pltpu.roll(jnp.where(right_half, previous, x), 64, 1)

        z = z_sum[:, here]
        g0, g1, g2 = diffusion[0, :, here], diffusion[1, :, here], diffusion[2, :, here]
        gt = ghosts[7:8, here]
        h0 = 0.5 * (flow[0, :, here] + g0 * (z - below_of(z, ghosts[2:3, here])))
        ht = 0.5 * (ghosts[6:7, here] + gt * (ghosts[5:6, here] - z[LAYERS - 1 :]))
        h1 = 0.5 * (flow[1, :, here] + g1 * (z - before_of(z, z_sum[:, back])))
        h2 = 0.5 * (flow[2, :, here] + g2 * (z - pltpu.roll(z, 1, 1)))
        h1, g1 = jnp.where(beyond_wall, h1, 0.0), jnp.where(beyond_wall, g1, 0.0)
        h2, g2 = jnp.where(inside, h2, 0.0), jnp.where(inside, g2, 0.0)
        half_inv = STEP * inv_volume[:, here]
        src = source[pl.ds(pl.multiple_of(i * LAYERS, LAYERS), LAYERS), :]
        onward = []
        for s in range(2):
            y = species[s, :, here]
            top = ghosts[3 + s : 4 + s, here]
            last = y[LAYERS - 1 :]
            y0 = below_of(y, ghosts[s : s + 1, here])
            y1 = before_of(y, species[s, :, back])
            y2 = pltpu.roll(y, 1, 1)
            f0 = h0 * (y + y0) - (g0 * d[s]) * (y - y0)
            ft = ht * (top + last) - (gt * d[s]) * (top - last)
            f1 = h1 * (y + y1) - (g1 * d[s]) * (y - y1)
            f2 = h2 * (y + y2) - (g2 * d[s]) * (y - y2)
            u0 = jnp.where(layer == LAYERS - 1, ft, pltpu.roll(f0, LAYERS - 1, 0))
            u1 = pltpu.roll(jnp.where(right_half, f1, carry[s]), 64, 1)
            u2 = pltpu.roll(f2, 127, 1)
            divergence = (u0 - f0) + ((u1 - f1) + (u2 - f2))
            delta = fuel if s == 0 else 0.0
            out[s, :, here] = y + half_inv * (src * (delta - y) - divergence)
            onward.append(f1)
        return tuple(onward)

    carry = (jnp.zeros((LAYERS, 128), F32),) * 2
    writes = []
    for g in range(4):
        carry = lax.fori_loop(g * 8, g * 8 + 8, strip, carry, unroll=4)
        done = pl.ds((3 - g) * 1024, 1024)
        writes.append(pltpu.make_async_copy(out.at[:, :, done], new_species.at[:, :, done], out_sems.at[g]))
        writes[-1].start()
    for write in writes:
        write.wait()


def spec(space=pltpu.VMEM):
    return pl.BlockSpec(memory_space=space)


HBM = pl.BlockSpec(memory_space=pltpu.HBM)


def params(**kw):
    return pltpu.CompilerParams(vmem_limit_bytes=VMEM_LIMIT, **kw)


def shape(*dims):
    return jax.ShapeDtypeStruct(dims, F32)


def body(
    species, interface_normal_flow, face_diffusion, inv_volume, diffusivity, low_partner, high_partner,
    low_orient, high_orient, droplet_table, parcel_block, parcel_cell, parcel_live,
):
    pick, oriented, unoriented, spread = constants()
    dma = pltpu.SemaphoreType.DMA
    vm = lambda *dims: pltpu.VMEM(dims, F32)
    iv = lambda *dims: pltpu.VMEM(dims, jnp.int32)
    bv = lambda *dims: pltpu.VMEM(dims, BF16)
    z_sum, source, ghosts, parcels, change = pl.pallas_call(
        exchange_kernel,
        out_shape=(shape(NQ, 8, JK), shape(1024, 128), shape(8, JK), shape(NB, ROWS, 128), shape(NB * CAP, 128)),
        in_specs=[HBM] * 16,
        out_specs=(spec(),) * 5,
        scratch_shapes=[
            pltpu.SMEM((2,), F32), vm(2, LAYERS, JK), vm(3, LAYERS, JK), vm(8, JK), *[iv(1, 64)] * 4, vm(256, 128), *[iv(1, 256)] * 3,
            bv(512, 64), bv(64, 1024), bv(64, 1024), bv(128, 1024),
            vm(NB, ROWS, 128), vm(NB, ROWS, 128), vm(NB, ROWS, 128), vm(NQ, NB, ROWS, 128),
            vm(NQ, 8, JK), vm(3, 8, JK), vm(8, JK), vm(8, 256), vm(8, 256), bv(1024, 1536),
            dma((16,)), dma((2 * CHUNKS + 1, 3)), dma((2 * CHUNKS + 1, 3)), dma((2,)), dma((2,)), dma((4,)), dma((3,)), dma,
        ],
        compiler_params=params(collective_id=0, has_side_effects=True),
        name="exchange",
    )(*(pltpu.with_memory_space_constraint(x, pltpu.HBM) for x in (
        diffusivity, species, interface_normal_flow, face_diffusion, low_partner, high_partner, low_orient, high_orient,
        droplet_table, parcel_block.reshape(1, -1), parcel_cell.reshape(1, -1), parcel_live.reshape(1, -1),
        pick, oriented, unoriented, spread,
    )))
    new_species, arrived = pl.pallas_call(
        final_kernel,
        out_shape=(shape(2, LAYERS, JK), shape(384, 128)),
        in_specs=[pl.BlockSpec(memory_space=pltpu.SMEM)] + [spec()] * 9,
        out_specs=(HBM, spec()),
        scratch_shapes=[vm(2, LAYERS, JK), dma((4,))],
        compiler_params=params(),
        name="final",
    )(
        diffusivity, species, interface_normal_flow, face_diffusion, inv_volume, z_sum.reshape(LAYERS, JK), source, ghosts,
        parcels.reshape(NB * ROWS, 128), change,
    )
    return new_species, arrived


def solution(mesh):
    placed = (
        P("sp", "blk", None), P(None, "blk", None), P(None, "blk", None), P("blk", None), P("sp"),
        P("blk", None), P("blk", None), P("blk", None), P("blk", None),
        P(("blk", "sp"), None), P(("blk", "sp"), None), P(("blk", "sp")), P(("blk", "sp")),
    )
    return jax.shard_map(
        body, mesh=mesh, in_specs=placed, out_specs=(P("sp", "blk", None), P(("blk", "sp"), None)), check_vma=False,
    )
```

time: 66.1 us -> 43.6 us (0.66)
  the two profiles are of different devices: /device:TPU:2 before, /device:TPU:1 now
where the time goes in v2:
time: 43.6 us; the launch traced here: 43.5 us
  Pallas kernels  42.7 us (98%)
  between operations  0.72 us (2%)
    pallas_call x1, Pallas kernels, body(): pl.pallas_call(exchange_kernel, out_shape=(shape(NQ, 8, JK), shape(1024,...  37.9 us
    pallas_call x1, Pallas kernels, body(): pl.pallas_call(final_kernel, out_shape=(shape(2, LAYERS, JK), shape(384,...  4.83 us

profile of v2, /device:TPU:1, one launch (start us, length us, event | category | flops | bytes accessed | tf_op | source)
XLA Modules:
  0.0 43.5 jit_solution(16281969899255878080)
XLA Ops:
  0.6 0.0 copy-start
  0.6 0.0 copy-start.1
  0.7 0.0 copy-start.2
  0.7 0.0 copy-start.3
  0.7 0.0 copy-start.4
  0.7 37.9 %exchange.1 = (f32[4,8,4096]{2,1,0:T(8,128)S(1)}, f32[1024,128]{1,0:T(8,128)S(1)}, f32[8,4096]{1,0:T(8,128)S(1)}, f32[64,8,128]{2,1,0:T(8,128)S(1)}, f32[384,128]{1,0:T(8,128)S(1)}) custom-call(f32[2]{0:T(128)} %dif.1, f32[2,32,4096]{2,1,0:T(8,128)} %species.1, f32[3,32,4096]{2,1,0:T(8,128)} %flow.1, f32[3,32,4096]{2,1,0:T(8,128)} %diffusion.1, ...), custom_call_target="tpu_custom_call" | custom-call | tf_op jit(solution)/shard_map/exchange/pallas_call | solution.py:466
  38.6 0.0 copy-done
  38.6 0.0 copy-done.1
  38.6 0.0 copy-done.2
  38.6 0.0 copy-done.3
  38.6 0.0 copy-done.4
  38.7 4.8 %final.1 = (f32[2,32,4096]{2,1,0:T(8,128)}, f32[384,128]{1,0:T(8,128)}) custom-call(f32[2]{0:T(128)S(1)} %copy-done.4, f32[2,32,4096]{2,1,0:T(8,128)S(1)} %copy-done.2, f32[3,32,4096]{2,1,0:T(8,128)S(1)} %copy-done, f32[3,32,4096]{2,1,0:T(8,128)S(1)} %copy-done.1, f32[32,4096]{1,0:T(8,128)S(1)} %copy-done.3, f32[32,4096]{1,0:T(8,128)S(1)} %bitcast.5, ...), custom_call_target="tpu_custom_call" | custom-call | tf_op jit(solution)/shard_map/final/pallas_call | solution.py:485
Async XLA Ops:
  0.6 38.0 %copy-start = (f32[3,32,4096]{2,1,0:T(8,128)S(1)}, f32[3,32,4096]{2,1,0:T(8,128)}, u32[]{:S(2)}) copy-start(f32[3,32,4096]{2,1,0:T(8,128)} %flow.1) | copy-start | bytes 4718596
  0.6 38.0 %copy-start.1 = (f32[3,32,4096]{2,1,0:T(8,128)S(1)}, f32[3,32,4096]{2,1,0:T(8,128)}, u32[]{:S(2)}) copy-start(f32[3,32,4096]{2,1,0:T(8,128)} %diffusion.1) | copy-start | bytes 4718596
  0.7 38.0 %copy-start.2 = (f32[2,32,4096]{2,1,0:T(8,128)S(1)}, f32[2,32,4096]{2,1,0:T(8,128)}, u32[]{:S(2)}) copy-start(f32[2,32,4096]{2,1,0:T(8,128)} %species.1) | copy-start | bytes 3145732
  0.7 38.0 %copy-start.3 = (f32[32,4096]{1,0:T(8,128)S(1)}, f32[32,4096]{1,0:T(8,128)}, u32[]{:S(2)}) copy-start(f32[32,4096]{1,0:T(8,128)} %inv_volume.1) | copy-start | bytes 1572868
  0.7 38.0 %copy-start.4 = (f32[2]{0:T(128)S(1)}, f32[2]{0:T(128)}, u32[]{:S(2)}) copy-start(f32[2]{0:T(128)} %dif.1) | copy-start | bytes 28

commit v3 on v2

v3 whole, which is shorter than its diff:
```python
import functools
import jax
import jax.numpy as jnp
import numpy as np
from jax import lax
from jax.experimental import pallas as pl
from jax.experimental.pallas import tpu as pltpu
from jax.sharding import PartitionSpec as P

NB = 64
NQ = 4
CAP = 6
ROWS = 8
CHUNKS = 2
NY = 4
NW = 16
LAYERS = 32
JK = 4096
MESH = pl.DeviceIdType.MESH
F32 = jnp.float32
BF16 = jnp.bfloat16
STEP = 0.5
DRAG = 0.3
VMEM_LIMIT = 36 * 1024 * 1024


def constants():
    lane = np.arange(512)
    cell = np.arange(64)
    pick = (lane[:, None] // 64 == cell[None, :] // 8) & (lane[:, None] % 8 == cell[None, :] % 8)
    r, c = cell // 8, cell % 8
    oriented, unoriented = [], []
    for code in range(8):
        f_row = (lambda v: 7 - v) if code & 1 else (lambda v: v)
        f_col = (lambda v: 7 - v) if code & 2 else (lambda v: v)
        r2, c2 = f_row(r), f_col(c)
        source = c2 * 8 + r2 if code & 4 else r2 * 8 + c2
        oriented += [cell[:, None] == source[None, :]] * 2
        source = f_row(c) * 8 + f_col(r) if code & 4 else f_row(r) * 8 + f_col(c)
        unoriented += [cell[:, None] == source[None, :]] * 2
    spread = np.zeros((128, 1024), bool)
    spread[:64, :512] = pick.T
    spread[64:, 512:] = pick.T
    pick3 = np.zeros((1536, 192), bool)
    for k in range(3):
        pick3[k * 512 : (k + 1) * 512, k * 64 : (k + 1) * 64] = pick
    thrice = lambda m: np.concatenate([m] * 3, 0)
    asb = lambda m: jnp.asarray(m.astype(np.float32), BF16)
    return asb(pick3), asb(thrice(np.concatenate(oriented, 1))), asb(thrice(np.concatenate(unoriented, 1))), asb(thrice(spread))


def pieces(x):
    hi = x.astype(BF16)
    rest = x - hi.astype(F32)
    mid = rest.astype(BF16)
    low = (rest - mid.astype(F32)).astype(BF16)
    return hi, mid, low


def mm(a, b):
    return lax.dot_general(a, b, (((1,), (0,)), ((), ())), preferred_element_type=F32)


def beside(x):
    return jnp.concatenate(pieces(x), axis=1)


def folded(x, n):
    return (x[:, :n] + x[:, n : 2 * n]) + x[:, 2 * n :]


def pick_rows(onehot, x):
    return folded(mm(onehot, beside(x)), x.shape[1])


def iota(shape, axis):
    return lax.broadcasted_iota(jnp.int32, shape, axis)


def ones(mask):
    return jnp.where(mask, 1.0, 0.0).astype(BF16)


def column(row):
    n = row.shape[1]
    return jnp.sum(jnp.where(iota((n, n), 0) == iota((n, n), 1), row, 0.0), axis=1, keepdims=True)


def strip_mask():
    lane = iota((8, 512), 1)
    return (lane % 64) // 8 == iota((8, 512), 0)


def stack_field(ref_slice):
    return jnp.concatenate([ref_slice[:, i * 128 : (i + 1) * 128] for i in range(LAYERS)], axis=0)


def lookups(cells, fields, ks):
    n = cells.shape[0]
    whole = cells.astype(jnp.int32)
    row = ((whole & 4095) >> 7) * LAYERS + (whole >> 12)
    hot = ones(iota((n, 1024), 1) == row)
    here = iota((n, 128), 1) == (whole & 127)
    for k in ks:
        yield jnp.sum(jnp.where(here, folded(mm(hot, fields[k]), 128), 0.0), axis=1, keepdims=True)


def ranks(block, live):
    n = block.shape[1]
    alive = live[...] == 1
    target = block[...].astype(F32)
    key = jnp.where(alive, target, -1.0)
    key_col = column(key)
    same = key_col == key
    first, second = iota((n, n), 0), iota((n, n), 1)
    rank = jnp.sum(jnp.where(same & (first < second), 1.0, 0.0), axis=0, keepdims=True)
    rank_col = jnp.sum(jnp.where(same & (second < first), 1.0, 0.0), axis=1, keepdims=True)
    return jnp.where(alive, target * ROWS, -1.0), jnp.where(alive, target * ROWS + rank, -1.0), rank_col


def meta_rows(table, cell, rank_col):
    rows = table[...]
    lane = iota(rows.shape, 1)
    cell_col = column(cell[...].astype(F32))
    boil = jnp.maximum(rows, 0.0) + jnp.log1p(jnp.exp(-jnp.abs(rows)))
    sig = 1.0 / (1.0 + jnp.exp(-rows))
    kind = lane & 7
    meta = jnp.where(kind == 0, cell_col, jnp.where(kind == 1, boil[:, 1:2], jnp.where(kind == 2, sig[:, 2:3], jnp.where(kind == 3, 1.0, 0.0))))
    return jnp.where((lane >> 3).astype(F32) == rank_col, meta, 0.0)


def turned_tiles(faces, pick, oriented, unoriented, high_code, low_code):
    mask = strip_mask()
    strips = []
    for face in faces:
        for jt in range(8):
            strips.append(jnp.where(mask, face[:, jt * 512 : (jt + 1) * 512], 0.0))
    tiles = mm(beside(jnp.concatenate(strips, axis=0)), pick[...]).astype(BF16)
    turned = mm(tiles[:128], oriented[...])
    unturned = mm(tiles[128:], unoriented[...])

    def choose(x, code):
        out = x[:, :128]
        for o in range(1, 8):
            out = jnp.where(code == o, x[:, o * 128 : (o + 1) * 128], out)
        return out

    return [choose(turned[k * 64 : (k + 1) * 64], high_code) for k in range(2)] + [
        choose(unturned[k * 64 : (k + 1) * 64], low_code) for k in range(4)
    ]


def addressed(keys, values, out):
    keys, values = jnp.concatenate(keys, axis=1), jnp.concatenate(values, axis=0)
    out[...] = pick_rows(ones(iota((NB * ROWS, keys.shape[1]), 0).astype(F32) == keys), values)


def exchange_kernel(
    dif_in, species_in, flow_in, diffusion_in, lp_in, hp_in, lo_in, ho_in, table_in, block_in, cell_in, live_in,
    pick_in, oriented_in, unoriented_in, spread_in,
    z_sum, source, ghosts, parcels, change,
    dif, species, flow, edge, lp, hp, lo, ho, table, block, cell, live, pick, oriented, unoriented, spread,
    msg_a, msg_b, mid_a, mid_b, recv_a, forward, z_part, z_got, z_mine, fuel, fuel_col, fields, hot,
    load_sems, sems, recv_sems, near_send, near_recv, wide_send, wide_recv, local_sems, fuel_send, fuel_recv,
):
    b, q = lax.axis_index("blk"), lax.axis_index("sp")
    y, w = lax.div(b, NW), lax.rem(b, NW)
    pairs = (
        (species_in, species), (dif_in, dif), (flow_in.at[0, pl.ds(0, 8)], edge.at[0]), (diffusion_in.at[0, pl.ds(0, 8)], edge.at[1]),
        (table_in, table), (block_in, block), (live_in, live), (cell_in, cell), (lp_in, lp), (hp_in, hp), (lo_in, lo), (ho_in, ho),
        (pick_in, pick), (oriented_in, oriented), (unoriented_in, unoriented), (flow_in, flow), (spread_in, spread),
    )
    loads = [pltpu.make_async_copy(src, dst, load_sems.at[k]) for k, (src, dst) in enumerate(pairs)]
    for load in loads:
        load.start()
    barrier = pltpu.get_barrier_semaphore()

    for d in range(1, NQ):
        pl.semaphore_signal(barrier, inc=1, device_id=(b, lax.rem(q + d, NQ)), device_id_type=MESH)
    for d in range(1, NY):
        pl.semaphore_signal(barrier, inc=1, device_id=(lax.rem(y + d, NY) * NW + w, q), device_id_type=MESH)
    for d in range(1, NW):
        pl.semaphore_signal(barrier, inc=1, device_id=(y * NW + lax.rem(w + d, NW), q), device_id_type=MESH)
    for load in loads[:15]:
        load.wait()

    d0, d1 = dif[0], dif[1]
    for k in range(NQ):
        z_part[k] = d0 * species[0, k * 8 : (k + 1) * 8] + d1 * species[1, k * 8 : (k + 1) * 8]
    to_block, to_slot, rank_col = ranks(block, live)
    up0, up1, lo0, lo1, fl, df = turned_tiles(
        [
            species[0, LAYERS - 1 : LAYERS, :], species[1, LAYERS - 1 : LAYERS, :], species[0, 0:1, :], species[1, 0:1, :],
            edge[0, 0:1, :], edge[1, 0:1, :],
        ],
        pick, oriented, unoriented, column(ho[...].astype(F32)), column(lo[...].astype(F32)),
    )
    left = iota((NB, 128), 1) < 64
    high, low = hp[...].astype(F32) * ROWS, lp[...].astype(F32) * ROWS
    addressed(
        [to_block, high + 1.0, low + 1.0, low + 2.0],
        [
            meta_rows(table, cell, rank_col), jnp.where(left, d0 * up0 + d1 * up1, 0.0), jnp.where(left, 0.0, d0 * lo0 + d1 * lo1),
            jnp.where(left, fl, df),
        ],
        msg_a.reshape(NB * ROWS, 128),
    )
    pl.semaphore_wait(barrier, NQ + NY + NW - 3)

    def sp_copy(src, dst, k, d):
        return pltpu.make_async_remote_copy(
            src_ref=src, dst_ref=dst, send_sem=sems.at[k, d - 1], recv_sem=recv_sems.at[k, d - 1],
            device_id=(b, lax.rem(q + d, NQ)), device_id_type=MESH,
        )

    wide = JK // CHUNKS
    part = [pl.ds(c * wide, wide) for c in range(CHUNKS)]
    scatter = [
        [sp_copy(z_part.at[lax.rem(q + d, NQ), :, part[c]], z_got.at[d - 1, :, part[c]], c, d) for d in (2, 1, 3)]
        for c in range(CHUNKS)
    ]
    gather = [
        [sp_copy(z_mine.at[:, part[c]], z_sum.at[q, :, part[c]], CHUNKS + c, d) for d in (2, 1, 3)] for c in range(CHUNKS)
    ]

    rows_a, rows_b = pl.ds(0, 3), pl.ds(0, ROWS)

    def along_y(msg, mid, rows, k):
        copies = []
        for d in (2, 1, 3):
            to = lax.rem(y + d, NY)
            copies.append(
                pltpu.make_async_remote_copy(
                    src_ref=msg.at[pl.ds(to * NW, NW), rows], dst_ref=mid.at[y, :, rows],
                    send_sem=near_send.at[k, d - 1], recv_sem=near_recv.at[k, d - 1],
                    device_id=(to * NW + w, q), device_id_type=MESH,
                )
            )
        keep = pltpu.make_async_copy(msg.at[pl.ds(y * NW, NW), rows], mid.at[y, :, rows], local_sems.at[2 * k])
        return copies, keep

    def across(mid, recv, rows, k):
        def step(d, carry):
            to = lax.rem(w + 1 + lax.rem(d + 7, NW - 1), NW)
            pltpu.make_async_remote_copy(
                src_ref=mid.at[:, to, rows], dst_ref=recv.at[:, w, rows], send_sem=wide_send.at[k], recv_sem=wide_recv.at[k],
                device_id=(y * NW + to, q), device_id_type=MESH,
            ).start()
            return carry

        lax.fori_loop(0, NW - 1, step, 0)
        keep = pltpu.make_async_copy(mid.at[:, w, rows], recv.at[:, w, rows], local_sems.at[2 * k + 1])
        keep.start()
        return keep

    most = pl.ds(0, NW - 1)
    first_a, keep_a = along_y(msg_a, mid_a, rows_a, 0)
    keep_a.start()
    for copy in first_a:
        copy.start()
    for copies in scatter:
        for copy in copies:
            copy.start()

    loads[15].wait()
    loads[16].wait()

    def cut(i, carry):
        here = pl.ds(pl.multiple_of(i * 128, 128), 128)
        there = pl.ds(pl.multiple_of(i * LAYERS, LAYERS), LAYERS)
        fields[0, there, :] = beside(species[0, :, here])
        for k in range(3):
            fields[k + 1, there, :] = beside(flow[k, :, here])
        return carry

    lax.fori_loop(0, LAYERS // 2, cut, 0, unroll=2)
    keep_a.wait()
    for copy in first_a:
        copy.wait_recv()
    keep_a = across(mid_a, recv_a, rows_a, 0)
    lax.fori_loop(LAYERS // 2, LAYERS, cut, 0, unroll=2)
    addressed(
        [to_slot, high + 6.0, low + 7.0],
        [table[...], jnp.where(left, up0, up1), jnp.where(left, lo0, lo1)],
        msg_b.reshape(NB * ROWS, 128),
    )
    first_b, keep_b = along_y(msg_b, mid_b, rows_b, 1)
    keep_b.start()
    for copy in first_b:
        copy.start()

    def gather_part(c):
        for copy in scatter[c]:
            copy.wait_recv()
        total = (z_part[q, :, part[c]] + z_got[0, :, part[c]]) + (z_got[1, :, part[c]] + z_got[2, :, part[c]])
        z_mine[:, part[c]] = total
        for copy in gather[c]:
            copy.start()
        z_sum[q, :, part[c]] = total

    keep_a.wait()
    pltpu.make_async_copy(recv_a.at[:, most, rows_a], recv_a.at[:, most, rows_a], wide_recv.at[0]).wait()
    two = pl.ds(0, 2)
    onward = [sp_copy(recv_a.at[:, :, two], forward.at[q, :, :, two], 2 * CHUNKS, d) for d in (2, 1, 3)]
    for copy in onward:
        copy.start()
    keep_f = pltpu.make_async_copy(recv_a.at[:, :, two], forward.at[q, :, :, two], local_sems.at[4])
    keep_f.start()
    gather_part(0)

    keep_b.wait()
    for copy in first_b:
        copy.wait_recv()
    keep_b = across(mid_b, parcels, rows_b, 1)

    got = recv_a.reshape(NB * ROWS, 128)
    got_b = parcels.reshape(NB * ROWS, 128)
    seen = forward.reshape(NQ * NB * ROWS, 128)
    own = got[pl.ds(0, NB, stride=ROWS), :]
    own_cells = jnp.concatenate([own[:, 8 * r : 8 * r + 1] for r in range(CAP)], axis=0)
    speeds = list(lookups(own_cells, fields, (1, 2, 3)))

    @pl.when(q != 0)
    def _():
        for c in range(1, CHUNKS):
            gather_part(c)

    keep_f.wait()
    for copy in onward:
        copy.wait_recv()
    meta = seen[pl.ds(0, NB * NQ, stride=ROWS), :]
    shared = [
        pltpu.make_async_remote_copy(
            src_ref=fuel, dst_ref=fuel, send_sem=fuel_send.at[d - 1], recv_sem=fuel_recv, device_id=(b, d), device_id_type=MESH
        )
        for d in (2, 1, 3)
    ]

    @pl.when(q == 0)
    def _():
        lane = iota((NB * NQ, 128), 1)
        found = jnp.zeros((NB * NQ, 128), F32)
        cells = jnp.concatenate([meta[:, 8 * r : 8 * r + 1] for r in range(CAP)], axis=0)
        [value] = lookups(cells, fields, (0,))
        for r in range(CAP):
            found = jnp.where(lane == r, value[r * NB * NQ : (r + 1) * NB * NQ], found)
        fuel[...] = jnp.transpose(found)[:8]
        for copy in shared:
            copy.start()
        for c in range(1, CHUNKS):
            gather_part(c)

    meta_t = jnp.transpose(meta)
    cells = jnp.concatenate([meta_t[8 * r : 8 * r + 1, :] for r in range(CAP)], axis=1).astype(jnp.int32)
    row = ((cells & 4095) >> 7) * LAYERS + (cells >> 12)
    for m in range(4):
        hot[m * 256 : (m + 1) * 256, :] = ones(iota((256, NB * NQ * CAP), 0) + m * 256 == row)

    def fill_ghosts():
        keep_b.wait()
        pltpu.make_async_copy(parcels.at[:, most], parcels.at[:, most], wide_recv.at[1]).wait()
        low_sel = ones(iota((NB, NB), 1).astype(F32) == column(lp[...].astype(F32)))
        high_sel = ones(iota((NB, NB), 1).astype(F32) == column(hp[...].astype(F32)))
        z_tiles = seen[pl.ds(1, NB * NQ, stride=ROWS), :]
        z_tiles = (z_tiles[:64] + z_tiles[64:128]) + (z_tiles[128:192] + z_tiles[192:])
        below = pick_rows(low_sel, jnp.concatenate([got_b[pl.ds(6, NB, stride=ROWS), :], z_tiles], axis=1))
        above = pick_rows(
            high_sel, jnp.concatenate([got_b[pl.ds(7, NB, stride=ROWS), :], got[pl.ds(2, NB, stride=ROWS), :], z_tiles], axis=1)
        )
        tiles = jnp.concatenate([below[:, :128], above[:, :128], above[:, 128:256], jnp.where(left, below[:, 128:], above[:, 256:])], axis=0)
        spread_tiles = mm(beside(tiles), spread[...])
        mask = strip_mask()
        slots = ((0, 1), (3, 4), (6, 7), (2, 5))
        for g in range(4):
            for jt in range(8):
                strip = spread_tiles[g * 64 + jt * 8 : g * 64 + jt * 8 + 8]
                for side in range(2):
                    value = jnp.sum(jnp.where(mask, strip[:, side * 512 : (side + 1) * 512], 0.0), axis=0, keepdims=True)
                    ghosts[slots[g][side] : slots[g][side] + 1, jt * 512 : (jt + 1) * 512] = value

    fill_ghosts()

    @pl.when(q != 0)
    def _():
        shared[0].wait_recv()

    found_col = jnp.transpose(jnp.concatenate([fuel[...], jnp.zeros((120, NB * NQ), F32)], axis=0))
    fuel_col[...] = found_col
    lane = iota((NB * NQ, 128), 1)
    mass = []
    for r in range(CAP):
        k = 8 * r
        gone = meta[:, k + 1 : k + 2] * (meta[:, k + 2 : k + 3] - found_col[:, r : r + 1])
        at = meta[:, k : k + 1].astype(jnp.int32) & 127
        mass.append(beside(jnp.where(lane == at, gone, 0.0)))
    source[...] = folded(mm(hot[...], jnp.concatenate(mass, axis=0)), 128)

    own_fuel = fuel_col[pl.ds(pl.multiple_of(q * NB, NB), NB), :]
    lane = iota((NB, 128), 1)
    for r in range(CAP):
        k = 8 * r
        gone = own[:, k + 1 : k + 2] * (own[:, k + 2 : k + 3] - own_fuel[:, r : r + 1])
        drag = DRAG * own[:, k + 3 : k + 4]
        moved = jnp.where(lane == 0, -gone, 0.0)
        for c in range(3):
            moved = jnp.where(lane == 3 + c, drag * speeds[c][r * NB : (r + 1) * NB], moved)
        change[pl.ds(r, NB, stride=CAP), :] = moved

    @pl.when(q == 0)
    def _():
        for copy in shared:
            copy.wait_send()

    pltpu.make_async_copy(mid_a.at[:, most, rows_a], mid_a.at[:, most, rows_a], wide_send.at[0]).wait()
    pltpu.make_async_copy(mid_b.at[:, most], mid_b.at[:, most], wide_send.at[1]).wait()
    for copy in first_a + first_b:
        copy.wait_send()
    for copies in scatter:
        for copy in copies:
            copy.wait_send()
    for copy in onward:
        copy.wait_send()
    for copies in gather:
        for copy in copies:
            copy.wait()


def final_kernel(
    dif, species, flow, diffusion, inv_volume, z_sum, source, ghosts, parcels, change, new_species, arrived, out, out_sems,
):
    q = lax.axis_index("sp")
    d = (dif[0], dif[1])
    lane = iota((NB, 128), 1)
    keep = jnp.where((lane >= 3) & (lane <= 5), 1.0 - DRAG, 1.0)
    for r in range(CAP):
        arrived[pl.ds(r, NB, stride=CAP), :] = parcels[pl.ds(r, NB, stride=ROWS), :] * keep + change[pl.ds(r, NB, stride=CAP), :]

    lane = iota((LAYERS, 128), 1)
    layer = iota((LAYERS, 128), 0)
    fuel = jnp.where(q == 0, 1.0, 0.0)
    right_half = lane >= 64
    inside = (lane & 63) != 0

    def strip(n, carry):
        i = LAYERS - 1 - n
        here = pl.ds(pl.multiple_of(i * 128, 128), 128)
        back = pl.ds(pl.multiple_of(jnp.maximum(i - 1, 0) * 128, 128), 128)
        beyond_wall = (i > 0) | right_half

        def below_of(x, ghost):
            return jnp.where(layer == 0, ghost, pltpu.roll(x, 1, 0))

        def before_of(x, previous):
            return pltpu.roll(jnp.where(right_half, previous, x), 64, 1)

        z = z_sum[:, here]
        g0, g1, g2 = diffusion[0, :, here], diffusion[1, :, here], diffusion[2, :, here]
        gt = ghosts[7:8, here]
        h0 = 0.5 * (flow[0, :, here] + g0 * (z - below_of(z, ghosts[2:3, here])))
        ht = 0.5 * (ghosts[6:7, here] + gt * (ghosts[5:6, here] - z[LAYERS - 1 :]))
        h1 = 0.5 * (flow[1, :, here] + g1 * (z - before_of(z, z_sum[:, back])))
        h2 = 0.5 * (flow[2, :, here] + g2 * (z - pltpu.roll(z, 1, 1)))
        h1, g1 = jnp.where(beyond_wall, h1, 0.0), jnp.where(beyond_wall, g1, 0.0)
        h2, g2 = jnp.where(inside, h2, 0.0), jnp.where(inside, g2, 0.0)
        half_inv = STEP * inv_volume[:, here]
        src = source[pl.ds(pl.multiple_of(i * LAYERS, LAYERS), LAYERS), :]
        onward = []
        for s in range(2):
            y = species[s, :, here]
            top = ghosts[3 + s : 4 + s, here]
            last = y[LAYERS - 1 :]
            y0 = below_of(y, ghosts[s : s + 1, here])
            y1 = before_of(y, species[s, :, back])
            y2 = pltpu.roll(y, 1, 1)
            f0 = h0 * (y + y0) - (g0 * d[s]) * (y - y0)
            ft = ht * (top + last) - (gt * d[s]) * (top - last)
            f1 = h1 * (y + y1) - (g1 * d[s]) * (y - y1)
            f2 = h2 * (y + y2) - (g2 * d[s]) * (y - y2)
            u0 = jnp.where(layer == LAYERS - 1, ft, pltpu.roll(f0, LAYERS - 1, 0))
            u1 = pltpu.roll(jnp.where(right_half, f1, carry[s]), 64, 1)
            u2 = pltpu.roll(f2, 127, 1)
            divergence = (u0 - f0) + ((u1 - f1) + (u2 - f2))
            delta = fuel if s == 0 else 0.0
            out[s, :, here] = y + half_inv * (src * (delta - y) - divergence)
            onward.append(f1)
        return tuple(onward)

    carry = (jnp.zeros((LAYERS, 128), F32),) * 2
    writes = []
    for g in range(4):
        carry = lax.fori_loop(g * 8, g * 8 + 8, strip, carry, unroll=4)
        done = pl.ds((3 - g) * 1024, 1024)
        writes.append(pltpu.make_async_copy(out.at[:, :, done], new_species.at[:, :, done], out_sems.at[g]))
        writes[-1].start()
    for write in writes:
        write.wait()


def spec(space=pltpu.VMEM):
    return pl.BlockSpec(memory_space=space)


HBM = pl.BlockSpec(memory_space=pltpu.HBM)


def params(**kw):
    return pltpu.CompilerParams(vmem_limit_bytes=VMEM_LIMIT, **kw)


def shape(*dims):
    return jax.ShapeDtypeStruct(dims, F32)


def body(
    species, interface_normal_flow, face_diffusion, inv_volume, diffusivity, low_partner, high_partner,
    low_orient, high_orient, droplet_table, parcel_block, parcel_cell, parcel_live,
):
    pick, oriented, unoriented, spread = constants()
    dma = pltpu.SemaphoreType.DMA
    vm = lambda *dims: pltpu.VMEM(dims, F32)
    iv = lambda *dims: pltpu.VMEM(dims, jnp.int32)
    bv = lambda *dims: pltpu.VMEM(dims, BF16)
    z_sum, source, ghosts, parcels, change = pl.pallas_call(
        exchange_kernel,
        out_shape=(shape(NQ, 8, JK), shape(1024, 128), shape(8, JK), shape(NY, NW, ROWS, 128), shape(NB * CAP, 128)),
        in_specs=[HBM] * 16,
        out_specs=(spec(),) * 5,
        scratch_shapes=[
            pltpu.SMEM((2,), F32), vm(2, LAYERS, JK), vm(3, LAYERS, JK), vm(2, 8, JK), *[iv(1, 64)] * 4, vm(256, 128), *[iv(1, 256)] * 3,
            bv(1536, 192), bv(192, 1024), bv(192, 1024), bv(384, 1024),
            vm(NB, ROWS, 128), vm(NB, ROWS, 128), *[vm(NY, NW, ROWS, 128)] * 3, vm(NQ, NY, NW, ROWS, 128),
            vm(NQ, 8, JK), vm(3, 8, JK), vm(8, JK), vm(8, 256), vm(256, 128), bv(4, 1024, 384), bv(1024, 1536),
            dma((17,)), dma((2 * CHUNKS + 1, 3)), dma((2 * CHUNKS + 1, 3)), dma((2, 3)), dma((2, 3)), dma((2,)), dma((2,)), dma((5,)), dma((3,)), dma,
        ],
        compiler_params=params(collective_id=0, has_side_effects=True),
        name="exchange",
    )(*(pltpu.with_memory_space_constraint(x, pltpu.HBM) for x in (
        diffusivity, species, interface_normal_flow, face_diffusion, low_partner, high_partner, low_orient, high_orient,
        droplet_table, parcel_block.reshape(1, -1), parcel_cell.reshape(1, -1), parcel_live.reshape(1, -1),
        pick, oriented, unoriented, spread,
    )))
    new_species, arrived = pl.pallas_call(
        final_kernel,
        out_shape=(shape(2, LAYERS, JK), shape(384, 128)),
        in_specs=[pl.BlockSpec(memory_space=pltpu.SMEM)] + [spec()] * 9,
        out_specs=(HBM, spec()),
        scratch_shapes=[vm(2, LAYERS, JK), dma((4,))],
        compiler_params=params(),
        name="final",
    )(
        diffusivity, species, interface_normal_flow, face_diffusion, inv_volume, z_sum.reshape(LAYERS, JK), source, ghosts,
        parcels.reshape(NB * ROWS, 128), change,
    )
    return new_species, arrived


def solution(mesh):
    placed = (
        P("sp", "blk", None), P(None, "blk", None), P(None, "blk", None), P("blk", None), P("sp"),
        P("blk", None), P("blk", None), P("blk", None), P("blk", None),
        P(("blk", "sp"), None), P(("blk", "sp"), None), P(("blk", "sp")), P(("blk", "sp")),
    )
    return jax.shard_map(
        body, mesh=mesh, in_specs=placed, out_specs=(P("sp", "blk", None), P(("blk", "sp"), None)), check_vma=False,
    )
```

time: 43.6 us -> 39.2 us (0.90)
  the two profiles are of different devices: /device:TPU:1 before, /device:TPU:2 now
where the time goes in v3:
time: 39.2 us; the launch traced here: 39.1 us
  Pallas kernels  38.3 us (98%)
  between operations  0.72 us (2%)
    pallas_call x1, Pallas kernels, body(): pl.pallas_call(exchange_kernel, out_shape=(shape(NQ, 8, JK), shape(1024,...  33.5 us
    pallas_call x1, Pallas kernels, body(): pl.pallas_call(final_kernel, out_shape=(shape(2, LAYERS, JK), shape(384,...  4.83 us

profile of v3, /device:TPU:2, one launch (start us, length us, event | category | flops | bytes accessed | tf_op | source)
XLA Modules:
  0.0 39.1 jit_solution(2798958956913250003)
XLA Ops:
  0.6 0.0 copy-start
  0.6 0.0 copy-start.1
  0.7 0.0 copy-start.2
  0.7 0.0 copy-start.3
  0.7 0.0 copy-start.4
  0.7 33.5 %exchange.1 = (f32[4,8,4096]{2,1,0:T(8,128)S(1)}, f32[1024,128]{1,0:T(8,128)S(1)}, f32[8,4096]{1,0:T(8,128)S(1)}, f32[4,16,8,128]{3,2,1,0:T(8,128)S(1)}, f32[384,128]{1,0:T(8,128)S(1)}) custom-call(f32[2]{0:T(128)} %dif.1, f32[2,32,4096]{2,1,0:T(8,128)} %species.1, f32[3,32,4096]{2,1,0:T(8,128)} %flow.1, f32[3,32,4096]{2,1,0:T(8,128)} %diffusion.1, ...), custom_call_target="tpu_custom_call" | custom-call | tf_op jit(solution)/shard_map/exchange/pallas_call | solution.py:523
  34.2 0.0 copy-done
  34.2 0.0 copy-done.1
  34.2 0.0 copy-done.2
  34.2 0.0 copy-done.3
  34.2 0.0 copy-done.4
  34.2 4.8 %final.1 = (f32[2,32,4096]{2,1,0:T(8,128)}, f32[384,128]{1,0:T(8,128)}) custom-call(f32[2]{0:T(128)S(1)} %copy-done.4, f32[2,32,4096]{2,1,0:T(8,128)S(1)} %copy-done.2, f32[3,32,4096]{2,1,0:T(8,128)S(1)} %copy-done, f32[3,32,4096]{2,1,0:T(8,128)S(1)} %copy-done.1, f32[32,4096]{1,0:T(8,128)S(1)} %copy-done.3, f32[32,4096]{1,0:T(8,128)S(1)} %bitcast.5, ...), custom_call_target="tpu_custom_call" | custom-call | tf_op jit(solution)/shard_map/final/pallas_call | solution.py:542
Async XLA Ops:
  0.6 33.6 %copy-start = (f32[3,32,4096]{2,1,0:T(8,128)S(1)}, f32[3,32,4096]{2,1,0:T(8,128)}, u32[]{:S(2)}) copy-start(f32[3,32,4096]{2,1,0:T(8,128)} %flow.1) | copy-start | bytes 4718596
  0.6 33.6 %copy-start.1 = (f32[3,32,4096]{2,1,0:T(8,128)S(1)}, f32[3,32,4096]{2,1,0:T(8,128)}, u32[]{:S(2)}) copy-start(f32[3,32,4096]{2,1,0:T(8,128)} %diffusion.1) | copy-start | bytes 4718596
  0.7 33.6 %copy-start.2 = (f32[2,32,4096]{2,1,0:T(8,128)S(1)}, f32[2,32,4096]{2,1,0:T(8,128)}, u32[]{:S(2)}) copy-start(f32[2,32,4096]{2,1,0:T(8,128)} %species.1) | copy-start | bytes 3145732
  0.7 33.6 %copy-start.3 = (f32[32,4096]{1,0:T(8,128)S(1)}, f32[32,4096]{1,0:T(8,128)}, u32[]{:S(2)}) copy-start(f32[32,4096]{1,0:T(8,128)} %inv_volume.1) | copy-start | bytes 1572868
  0.7 33.6 %copy-start.4 = (f32[2]{0:T(128)S(1)}, f32[2]{0:T(128)}, u32[]{:S(2)}) copy-start(f32[2]{0:T(128)} %dif.1) | copy-start | bytes 28

commit v4 on v3

--- a/solution.py
+++ b/solution.py
@@ -14,6 +14,8 @@
 CHUNKS = 2
 NY = 4
 NW = 16
+CUT = 16
+KINDS = 3
 LAYERS = 32
 JK = 4096
 MESH = pl.DeviceIdType.MESH
@@ -160,7 +162,7 @@
     pick_in, oriented_in, unoriented_in, spread_in,
     z_sum, source, ghosts, parcels, change,
     dif, species, flow, edge, lp, hp, lo, ho, table, block, cell, live, pick, oriented, unoriented, spread,
-    msg_a, msg_b, mid_a, mid_b, recv_a, forward, z_part, z_got, z_mine, fuel, fuel_col, fields, hot,
+    msg_a, msg_b, mid_a, mid_b, pack_a, recv_a, forward, z_part, z_got, z_mine, fuel, fuel_col, fields, hot,
     load_sems, sems, recv_sems, near_send, near_recv, wide_send, wide_recv, local_sems, fuel_send, fuel_recv,
 ):
     b, q = lax.axis_index("blk"), lax.axis_index("sp")
@@ -181,12 +183,14 @@
         pl.semaphore_signal(barrier, inc=1, device_id=(lax.rem(y + d, NY) * NW + w, q), device_id_type=MESH)
     for d in range(1, NW):
         pl.semaphore_signal(barrier, inc=1, device_id=(y * NW + lax.rem(w + d, NW), q), device_id_type=MESH)
-    for load in loads[:15]:
-        load.wait()
+    loads[0].wait()
+    loads[1].wait()
 
     d0, d1 = dif[0], dif[1]
     for k in range(NQ):
         z_part[k] = d0 * species[0, k * 8 : (k + 1) * 8] + d1 * species[1, k * 8 : (k + 1) * 8]
+    for load in loads[2:15]:
+        load.wait()
     to_block, to_slot, rank_col = ranks(block, live)
     up0, up1, lo0, lo1, fl, df = turned_tiles(
         [
@@ -197,14 +201,16 @@
     )
     left = iota((NB, 128), 1) < 64
     high, low = hp[...].astype(F32) * ROWS, lp[...].astype(F32) * ROWS
-    addressed(
-        [to_block, high + 1.0, low + 1.0, low + 2.0],
-        [
-            meta_rows(table, cell, rank_col), jnp.where(left, d0 * up0 + d1 * up1, 0.0), jnp.where(left, 0.0, d0 * lo0 + d1 * lo1),
-            jnp.where(left, fl, df),
-        ],
-        msg_a.reshape(NB * ROWS, 128),
-    )
+    by_block = iota((NB, 256), 0).astype(F32) * ROWS == to_block
+    tile_keys = jnp.concatenate([high, low], axis=1)
+    by_tile = ones(iota((NB, 2 * NB), 0).astype(F32) * ROWS == tile_keys)
+    z_tiles = jnp.concatenate([jnp.where(left, d0 * up0 + d1 * up1, 0.0), jnp.where(left, 0.0, d0 * lo0 + d1 * lo1)], axis=0)
+    edges = jnp.concatenate([jnp.zeros((NB, 128), F32), jnp.where(left, fl, df)], axis=0)
+    picked = pick_rows(by_tile, jnp.concatenate([z_tiles, edges], axis=1))
+    kinds = (pick_rows(ones(by_block), meta_rows(table, cell, rank_col)), picked[:, :128], picked[:, 128:])
+    for k in range(KINDS):
+        for to in range(NY):
+            msg_a[to, k] = kinds[k][to * NW : (to + 1) * NW]
     pl.semaphore_wait(barrier, NQ + NY + NW - 3)
 
     def sp_copy(src, dst, k, d):
@@ -223,39 +229,31 @@
         [sp_copy(z_mine.at[:, part[c]], z_sum.at[q, :, part[c]], CHUNKS + c, d) for d in (2, 1, 3)] for c in range(CHUNKS)
     ]
 
-    rows_a, rows_b = pl.ds(0, 3), pl.ds(0, ROWS)
-
-    def along_y(msg, mid, rows, k):
+    def along_y(msg, mid, k):
         copies = []
         for d in (2, 1, 3):
             to = lax.rem(y + d, NY)
             copies.append(
                 pltpu.make_async_remote_copy(
-                    src_ref=msg.at[pl.ds(to * NW, NW), rows], dst_ref=mid.at[y, :, rows],
-                    send_sem=near_send.at[k, d - 1], recv_sem=near_recv.at[k, d - 1],
+                    src_ref=msg.at[to], dst_ref=mid.at[y], send_sem=near_send.at[k, d - 1], recv_sem=near_recv.at[k, d - 1],
                     device_id=(to * NW + w, q), device_id_type=MESH,
                 )
             )
-        keep = pltpu.make_async_copy(msg.at[pl.ds(y * NW, NW), rows], mid.at[y, :, rows], local_sems.at[2 * k])
-        return copies, keep
-
-    def across(mid, recv, rows, k):
+        return copies
+
+    def across(src, dst, k):
         def step(d, carry):
             to = lax.rem(w + 1 + lax.rem(d + 7, NW - 1), NW)
             pltpu.make_async_remote_copy(
-                src_ref=mid.at[:, to, rows], dst_ref=recv.at[:, w, rows], send_sem=wide_send.at[k], recv_sem=wide_recv.at[k],
+                src_ref=src(to), dst_ref=dst(w), send_sem=wide_send.at[k], recv_sem=wide_recv.at[k],
                 device_id=(y * NW + to, q), device_id_type=MESH,
             ).start()
             return carry
 
         lax.fori_loop(0, NW - 1, step, 0)
-        keep = pltpu.make_async_copy(mid.at[:, w, rows], recv.at[:, w, rows], local_sems.at[2 * k + 1])
-        keep.start()
-        return keep
 
     most = pl.ds(0, NW - 1)
-    first_a, keep_a = along_y(msg_a, mid_a, rows_a, 0)
-    keep_a.start()
+    first_a = along_y(msg_a, mid_a, 0)
     for copy in first_a:
         copy.start()
     for copies in scatter:
@@ -273,21 +271,36 @@
             fields[k + 1, there, :] = beside(flow[k, :, here])
         return carry
 
-    lax.fori_loop(0, LAYERS // 2, cut, 0, unroll=2)
-    keep_a.wait()
+    mid_a[y] = msg_a[y]
     for copy in first_a:
         copy.wait_recv()
-    keep_a = across(mid_a, recv_a, rows_a, 0)
-    lax.fori_loop(LAYERS // 2, LAYERS, cut, 0, unroll=2)
+    packed = pack_a.reshape(NW * NW, 128)
+    for src in range(NY):
+        for k in range(KINDS):
+            packed[pl.ds(src * KINDS + k, NW, stride=NW), :] = mid_a[src, k]
+    rows_a = pl.ds(0, NY * KINDS)
+    across(lambda to: pack_a.at[to, rows_a], lambda me: recv_a.at[me, rows_a], 0)
+    recv_a[w] = pack_a[w]
     addressed(
         [to_slot, high + 6.0, low + 7.0],
         [table[...], jnp.where(left, up0, up1), jnp.where(left, lo0, lo1)],
         msg_b.reshape(NB * ROWS, 128),
     )
-    first_b, keep_b = along_y(msg_b, mid_b, rows_b, 1)
+    keep_b = pltpu.make_async_copy(msg_b.at[y], mid_b.at[y], local_sems.at[0])
+    first_b = along_y(msg_b, mid_b, 1)
     keep_b.start()
     for copy in first_b:
         copy.start()
+
+    lax.fori_loop(0, CUT, cut, 0, unroll=2)
+    lax.fori_loop(CUT, LAYERS, cut, 0, unroll=2)
+
+    keep_b.wait()
+    for copy in first_b:
+        copy.wait_recv()
+    across(lambda to: mid_b.at[:, to], lambda me: parcels.at[:, me], 1)
+    keep_b = pltpu.make_async_copy(mid_b.at[:, w], parcels.at[:, w], local_sems.at[1])
+    keep_b.start()
 
     def gather_part(c):
         for copy in scatter[c]:
@@ -298,25 +311,19 @@
             copy.start()
         z_sum[q, :, part[c]] = total
 
-    keep_a.wait()
-    pltpu.make_async_copy(recv_a.at[:, most, rows_a], recv_a.at[:, most, rows_a], wide_recv.at[0]).wait()
-    two = pl.ds(0, 2)
-    onward = [sp_copy(recv_a.at[:, :, two], forward.at[q, :, :, two], 2 * CHUNKS, d) for d in (2, 1, 3)]
+    pltpu.make_async_copy(recv_a.at[most, rows_a], recv_a.at[most, rows_a], wide_recv.at[0]).wait()
+    got = recv_a.reshape(NW * NW, 128)
+    own, own_z, own_edges = (
+        jnp.concatenate([got[pl.ds(src * KINDS + k, NW, stride=NW), :] for src in range(NY)], axis=0) for k in range(KINDS)
+    )
+    forward[q, 0] = own
+    forward[q, 1] = own_z
+    onward = [sp_copy(forward.at[q], forward.at[q], 2 * CHUNKS, d) for d in (2, 1, 3)]
     for copy in onward:
         copy.start()
-    keep_f = pltpu.make_async_copy(recv_a.at[:, :, two], forward.at[q, :, :, two], local_sems.at[4])
-    keep_f.start()
     gather_part(0)
 
-    keep_b.wait()
-    for copy in first_b:
-        copy.wait_recv()
-    keep_b = across(mid_b, parcels, rows_b, 1)
-
-    got = recv_a.reshape(NB * ROWS, 128)
     got_b = parcels.reshape(NB * ROWS, 128)
-    seen = forward.reshape(NQ * NB * ROWS, 128)
-    own = got[pl.ds(0, NB, stride=ROWS), :]
     own_cells = jnp.concatenate([own[:, 8 * r : 8 * r + 1] for r in range(CAP)], axis=0)
     speeds = list(lookups(own_cells, fields, (1, 2, 3)))
 
@@ -325,10 +332,9 @@
         for c in range(1, CHUNKS):
             gather_part(c)
 
-    keep_f.wait()
     for copy in onward:
         copy.wait_recv()
-    meta = seen[pl.ds(0, NB * NQ, stride=ROWS), :]
+    meta = jnp.concatenate([forward[k, 0] for k in range(NQ)], axis=0)
     shared = [
         pltpu.make_async_remote_copy(
             src_ref=fuel, dst_ref=fuel, send_sem=fuel_send.at[d - 1], recv_sem=fuel_recv, device_id=(b, d), device_id_type=MESH
@@ -361,11 +367,10 @@
         pltpu.make_async_copy(parcels.at[:, most], parcels.at[:, most], wide_recv.at[1]).wait()
         low_sel = ones(iota((NB, NB), 1).astype(F32) == column(lp[...].astype(F32)))
         high_sel = ones(iota((NB, NB), 1).astype(F32) == column(hp[...].astype(F32)))
-        z_tiles = seen[pl.ds(1, NB * NQ, stride=ROWS), :]
-        z_tiles = (z_tiles[:64] + z_tiles[64:128]) + (z_tiles[128:192] + z_tiles[192:])
+        z_tiles = (forward[0, 1] + forward[1, 1]) + (forward[2, 1] + forward[3, 1])
         below = pick_rows(low_sel, jnp.concatenate([got_b[pl.ds(6, NB, stride=ROWS), :], z_tiles], axis=1))
         above = pick_rows(
-            high_sel, jnp.concatenate([got_b[pl.ds(7, NB, stride=ROWS), :], got[pl.ds(2, NB, stride=ROWS), :], z_tiles], axis=1)
+            high_sel, jnp.concatenate([got_b[pl.ds(7, NB, stride=ROWS), :], own_edges, z_tiles], axis=1)
         )
         tiles = jnp.concatenate([below[:, :128], above[:, :128], above[:, 128:256], jnp.where(left, below[:, 128:], above[:, 256:])], axis=0)
         spread_tiles = mm(beside(tiles), spread[...])
@@ -411,7 +416,7 @@
         for copy in shared:
             copy.wait_send()
 
-    pltpu.make_async_copy(mid_a.at[:, most, rows_a], mid_a.at[:, most, rows_a], wide_send.at[0]).wait()
+    pltpu.make_async_copy(pack_a.at[most, rows_a], pack_a.at[most, rows_a], wide_send.at[0]).wait()
     pltpu.make_async_copy(mid_b.at[:, most], mid_b.at[:, most], wide_send.at[1]).wait()
     for copy in first_a + first_b:
         copy.wait_send()
@@ -426,14 +431,17 @@
 
 
 def final_kernel(
-    dif, species, flow, diffusion, inv_volume, z_sum, source, ghosts, parcels, change, new_species, arrived, out, out_sems,
+    dif, species, flow, diffusion, inv_volume, z_sum, source, ghosts, parcels, change, new_species, arrived, out, landed, out_sems,
 ):
     q = lax.axis_index("sp")
     d = (dif[0], dif[1])
     lane = iota((NB, 128), 1)
     keep = jnp.where((lane >= 3) & (lane <= 5), 1.0 - DRAG, 1.0)
     for r in range(CAP):
-        arrived[pl.ds(r, NB, stride=CAP), :] = parcels[pl.ds(r, NB, stride=ROWS), :] * keep + change[pl.ds(r, NB, stride=CAP), :]
+        landed[pl.ds(r, NB, stride=CAP), :] = parcels[pl.ds(r, NB, stride=ROWS), :] * keep + change[pl.ds(r, NB, stride=CAP), :]
+
+    writes = [pltpu.make_async_copy(landed, arrived, out_sems.at[0])]
+    writes[0].start()
 
     lane = iota((LAYERS, 128), 1)
     layer = iota((LAYERS, 128), 0)
@@ -486,11 +494,11 @@
         return tuple(onward)
 
     carry = (jnp.zeros((LAYERS, 128), F32),) * 2
-    writes = []
-    for g in range(4):
-        carry = lax.fori_loop(g * 8, g * 8 + 8, strip, carry, unroll=4)
-        done = pl.ds((3 - g) * 1024, 1024)
-        writes.append(pltpu.make_async_copy(out.at[:, :, done], new_species.at[:, :, done], out_sems.at[g]))
+    bounds = (0, 8, 16, 24, 28, 32)
+    for g in range(5):
+        carry = lax.fori_loop(bounds[g], bounds[g + 1], strip, carry, unroll=4)
+        done = pl.ds((LAYERS - bounds[g + 1]) * 128, (bounds[g + 1] - bounds[g]) * 128)
+        writes.append(pltpu.make_async_copy(out.at[:, :, done], new_species.at[:, :, done], out_sems.at[g + 1]))
         writes[-1].start()
     for write in writes:
         write.wait()
@@ -528,9 +536,10 @@
         scratch_shapes=[
             pltpu.SMEM((2,), F32), vm(2, LAYERS, JK), vm(3, LAYERS, JK), vm(2, 8, JK), *[iv(1, 64)] * 4, vm(256, 128), *[iv(1, 256)] * 3,
             bv(1536, 192), bv(192, 1024), bv(192, 1024), bv(384, 1024),
-            vm(NB, ROWS, 128), vm(NB, ROWS, 128), *[vm(NY, NW, ROWS, 128)] * 3, vm(NQ, NY, NW, ROWS, 128),
+            vm(NY, KINDS, NW, 128), vm(NY, NW, ROWS, 128), vm(NY, KINDS, NW, 128), vm(NY, NW, ROWS, 128), *[vm(NW, NW, 128)] * 2,
+            vm(NQ, 2, NB, 128),
             vm(NQ, 8, JK), vm(3, 8, JK), vm(8, JK), vm(8, 256), vm(256, 128), bv(4, 1024, 384), bv(1024, 1536),
-            dma((17,)), dma((2 * CHUNKS + 1, 3)), dma((2 * CHUNKS + 1, 3)), dma((2, 3)), dma((2, 3)), dma((2,)), dma((2,)), dma((5,)), dma((3,)), dma,
+            dma((17,)), dma((2 * CHUNKS + 1, 3)), dma((2 * CHUNKS + 1, 3)), dma((2, 3)), dma((2, 3)), dma((2,)), dma((2,)), dma((2,)), dma((3,)), dma,
         ],
         compiler_params=params(collective_id=0, has_side_effects=True),
         name="exchange",
@@ -543,8 +552,8 @@
         final_kernel,
         out_shape=(shape(2, LAYERS, JK), shape(384, 128)),
         in_specs=[pl.BlockSpec(memory_space=pltpu.SMEM)] + [spec()] * 9,
-        out_specs=(HBM, spec()),
-        scratch_shapes=[vm(2, LAYERS, JK), dma((4,))],
+        out_specs=(HBM, HBM),
+        scratch_shapes=[vm(2, LAYERS, JK), vm(NB * CAP, 128), dma((6,))],
         compiler_params=params(),
         name="final",
     )(

time: 39.2 us -> 38.2 us (0.974)
  Pallas kernels: 38.3 us -> 37.4 us
    pallas_call x1, Pallas kernels: 33.5 us -> 33 us  [body(): pl.pallas_call(exchange_kernel, out_shape=(shape(NQ, 8, JK), shape(1024,...]
    pallas_call x1, Pallas kernels: 4.83 us -> 4.43 us  [body(): pl.pallas_call(final_kernel, out_shape=(shape(2, LAYERS, JK), shape(384,...]
where the time goes in v4:
time: 38.2 us; the launch traced here: 38.1 us
  Pallas kernels  37.4 us (98%)
  between operations  0.72 us (2%)
    pallas_call x1, Pallas kernels, body(): pl.pallas_call(exchange_kernel, out_shape=(shape(NQ, 8, JK), shape(1024,...  33 us
    pallas_call x1, Pallas kernels, body(): pl.pallas_call(final_kernel, out_shape=(shape(2, LAYERS, JK), shape(384,...  4.43 us

profile of v4, /device:TPU:2, one launch (start us, length us, event | category | flops | bytes accessed | tf_op | source)
XLA Modules:
  0.0 38.1 jit_solution(17364132483823167887)
XLA Ops:
  0.6 0.0 copy-start
  0.6 0.0 copy-start.1
  0.7 0.0 copy-start.2
  0.7 0.0 copy-start.3
  0.7 0.0 copy-start.4
  0.7 33.0 %exchange.1 = (f32[4,8,4096]{2,1,0:T(8,128)S(1)}, f32[1024,128]{1,0:T(8,128)S(1)}, f32[8,4096]{1,0:T(8,128)S(1)}, f32[4,16,8,128]{3,2,1,0:T(8,128)S(1)}, f32[384,128]{1,0:T(8,128)S(1)}) custom-call(f32[2]{0:T(128)} %dif.1, f32[2,32,4096]{2,1,0:T(8,128)} %species.1, f32[3,32,4096]{2,1,0:T(8,128)} %flow.1, f32[3,32,4096]{2,1,0:T(8,128)} %diffusion.1, ...), custom_call_target="tpu_custom_call" | custom-call | tf_op jit(solution)/shard_map/exchange/pallas_call | solution.py:531
  33.7 0.0 copy-done
  33.7 0.0 copy-done.1
  33.7 0.0 copy-done.2
  33.7 0.0 copy-done.3
  33.7 0.0 copy-done.4
  33.7 4.4 %final.1 = (f32[2,32,4096]{2,1,0:T(8,128)}, f32[384,128]{1,0:T(8,128)}) custom-call(f32[2]{0:T(128)S(1)} %copy-done.4, f32[2,32,4096]{2,1,0:T(8,128)S(1)} %copy-done.2, f32[3,32,4096]{2,1,0:T(8,128)S(1)} %copy-done, f32[3,32,4096]{2,1,0:T(8,128)S(1)} %copy-done.1, f32[32,4096]{1,0:T(8,128)S(1)} %copy-done.3, f32[32,4096]{1,0:T(8,128)S(1)} %bitcast.5, ...), custom_call_target="tpu_custom_call" | custom-call | tf_op jit(solution)/shard_map/final/pallas_call | solution.py:551
Async XLA Ops:
  0.6 33.0 %copy-start = (f32[3,32,4096]{2,1,0:T(8,128)S(1)}, f32[3,32,4096]{2,1,0:T(8,128)}, u32[]{:S(2)}) copy-start(f32[3,32,4096]{2,1,0:T(8,128)} %flow.1) | copy-start | bytes 4718596
  0.6 33.0 %copy-start.1 = (f32[3,32,4096]{2,1,0:T(8,128)S(1)}, f32[3,32,4096]{2,1,0:T(8,128)}, u32[]{:S(2)}) copy-start(f32[3,32,4096]{2,1,0:T(8,128)} %diffusion.1) | copy-start | bytes 4718596
  0.7 33.0 %copy-start.2 = (f32[2,32,4096]{2,1,0:T(8,128)S(1)}, f32[2,32,4096]{2,1,0:T(8,128)}, u32[]{:S(2)}) copy-start(f32[2,32,4096]{2,1,0:T(8,128)} %species.1) | copy-start | bytes 3145732
  0.7 33.0 %copy-start.3 = (f32[32,4096]{1,0:T(8,128)S(1)}, f32[32,4096]{1,0:T(8,128)}, u32[]{:S(2)}) copy-start(f32[32,4096]{1,0:T(8,128)} %inv_volume.1) | copy-start | bytes 1572868
  0.7 33.0 %copy-start.4 = (f32[2]{0:T(128)S(1)}, f32[2]{0:T(128)}, u32[]{:S(2)}) copy-start(f32[2]{0:T(128)} %dif.1) | copy-start | bytes 28

commit v5 on v4

--- a/solution.py
+++ b/solution.py
@@ -162,7 +162,7 @@
     pick_in, oriented_in, unoriented_in, spread_in,
     z_sum, source, ghosts, parcels, change,
     dif, species, flow, edge, lp, hp, lo, ho, table, block, cell, live, pick, oriented, unoriented, spread,
-    msg_a, msg_b, mid_a, mid_b, pack_a, recv_a, forward, z_part, z_got, z_mine, fuel, fuel_col, fields, hot,
+    msg_a, msg_b, mid_a, mid_b, pack_a, recv_a, lists, forward, z_part, z_got, z_mine, fuel, fuel_col, fields, hot,
     load_sems, sems, recv_sems, near_send, near_recv, wide_send, wide_recv, local_sems, fuel_send, fuel_recv,
 ):
     b, q = lax.axis_index("blk"), lax.axis_index("sp")
@@ -316,10 +316,11 @@
     own, own_z, own_edges = (
         jnp.concatenate([got[pl.ds(src * KINDS + k, NW, stride=NW), :] for src in range(NY)], axis=0) for k in range(KINDS)
     )
-    forward[q, 0] = own
-    forward[q, 1] = own_z
-    onward = [sp_copy(forward.at[q], forward.at[q], 2 * CHUNKS, d) for d in (2, 1, 3)]
-    for copy in onward:
+    lists[q] = jnp.where(iota((NB // 2, 128), 1) < 64, own[: NB // 2], pltpu.roll(own[NB // 2 :], 64, 1))
+    forward[q] = own_z
+    onward = [sp_copy(lists.at[q], lists.at[q], 2 * CHUNKS, d) for d in (2, 1, 3)]
+    onward_z = [sp_copy(forward.at[q], forward.at[q], 2 * CHUNKS + 1, d) for d in (2, 1, 3)]
+    for copy in onward + onward_z:
         copy.start()
     gather_part(0)
 
@@ -334,7 +335,11 @@
 
     for copy in onward:
         copy.wait_recv()
-    meta = jnp.concatenate([forward[k, 0] for k in range(NQ)], axis=0)
+    meta = []
+    for k in range(NQ):
+        both = lists[k]
+        meta += [both, pltpu.roll(both, 64, 1)]
+    meta = jnp.concatenate(meta, axis=0)
     shared = [
         pltpu.make_async_remote_copy(
             src_ref=fuel, dst_ref=fuel, send_sem=fuel_send.at[d - 1], recv_sem=fuel_recv, device_id=(b, d), device_id_type=MESH
@@ -367,7 +372,9 @@
         pltpu.make_async_copy(parcels.at[:, most], parcels.at[:, most], wide_recv.at[1]).wait()
         low_sel = ones(iota((NB, NB), 1).astype(F32) == column(lp[...].astype(F32)))
         high_sel = ones(iota((NB, NB), 1).astype(F32) == column(hp[...].astype(F32)))
-        z_tiles = (forward[0, 1] + forward[1, 1]) + (forward[2, 1] + forward[3, 1])
+        for copy in onward_z:
+            copy.wait_recv()
+        z_tiles = (forward[0] + forward[1]) + (forward[2] + forward[3])
         below = pick_rows(low_sel, jnp.concatenate([got_b[pl.ds(6, NB, stride=ROWS), :], z_tiles], axis=1))
         above = pick_rows(
             high_sel, jnp.concatenate([got_b[pl.ds(7, NB, stride=ROWS), :], own_edges, z_tiles], axis=1)
@@ -423,7 +430,7 @@
     for copies in scatter:
         for copy in copies:
             copy.wait_send()
-    for copy in onward:
+    for copy in onward + onward_z:
         copy.wait_send()
     for copies in gather:
         for copy in copies:
@@ -537,9 +544,9 @@
             pltpu.SMEM((2,), F32), vm(2, LAYERS, JK), vm(3, LAYERS, JK), vm(2, 8, JK), *[iv(1, 64)] * 4, vm(256, 128), *[iv(1, 256)] * 3,
             bv(1536, 192), bv(192, 1024), bv(192, 1024), bv(384, 1024),
             vm(NY, KINDS, NW, 128), vm(NY, NW, ROWS, 128), vm(NY, KINDS, NW, 128), vm(NY, NW, ROWS, 128), *[vm(NW, NW, 128)] * 2,
-            vm(NQ, 2, NB, 128),
+            vm(NQ, NB // 2, 128), vm(NQ, NB, 128),
             vm(NQ, 8, JK), vm(3, 8, JK), vm(8, JK), vm(8, 256), vm(256, 128), bv(4, 1024, 384), bv(1024, 1536),
-            dma((17,)), dma((2 * CHUNKS + 1, 3)), dma((2 * CHUNKS + 1, 3)), dma((2, 3)), dma((2, 3)), dma((2,)), dma((2,)), dma((2,)), dma((3,)), dma,
+            dma((17,)), dma((2 * CHUNKS + 2, 3)), dma((2 * CHUNKS + 2, 3)), dma((2, 3)), dma((2, 3)), dma((2,)), dma((2,)), dma((2,)), dma((3,)), dma,
         ],
         compiler_params=params(collective_id=0, has_side_effects=True),
         name="exchange",

time: 38.2 us -> 36.3 us (0.950)
  Pallas kernels: 37.4 us -> 35.5 us
    pallas_call x1, Pallas kernels: 33 us -> 31.1 us  [body(): pl.pallas_call(exchange_kernel, out_shape=(shape(NQ, 8, JK), shape(1024,...]
where the time goes in v5:
time: 36.3 us
  Pallas kernels  35.5 us (98%)
  between operations  0.72 us (2%)
    pallas_call x1, Pallas kernels, body(): pl.pallas_call(exchange_kernel, out_shape=(shape(NQ, 8, JK), shape(1024,...  31.1 us
    pallas_call x1, Pallas kernels, body(): pl.pallas_call(final_kernel, out_shape=(shape(2, LAYERS, JK), shape(384,...  4.43 us

profile of v5, /device:TPU:2, one launch (start us, length us, event | category | flops | bytes accessed | tf_op | source)
XLA Modules:
  0.0 36.3 jit_solution(9886953569488347915)
XLA Ops:
  0.6 0.0 copy-start
  0.6 0.0 copy-start.1
  0.7 0.0 copy-start.2
  0.7 0.0 copy-start.3
  0.7 0.0 copy-start.4
  0.7 31.1 %exchange.1 = (f32[4,8,4096]{2,1,0:T(8,128)S(1)}, f32[1024,128]{1,0:T(8,128)S(1)}, f32[8,4096]{1,0:T(8,128)S(1)}, f32[4,16,8,128]{3,2,1,0:T(8,128)S(1)}, f32[384,128]{1,0:T(8,128)S(1)}) custom-call(f32[2]{0:T(128)} %dif.1, f32[2,32,4096]{2,1,0:T(8,128)} %species.1, f32[3,32,4096]{2,1,0:T(8,128)} %flow.1, f32[3,32,4096]{2,1,0:T(8,128)} %diffusion.1, ...), custom_call_target="tpu_custom_call" | custom-call | tf_op jit(solution)/shard_map/exchange/pallas_call | solution.py:538
  31.8 0.0 copy-done
  31.8 0.0 copy-done.1
  31.8 0.0 copy-done.2
  31.8 0.0 copy-done.3
  31.8 0.0 copy-done.4
  31.8 4.4 %final.1 = (f32[2,32,4096]{2,1,0:T(8,128)}, f32[384,128]{1,0:T(8,128)}) custom-call(f32[2]{0:T(128)S(1)} %copy-done.4, f32[2,32,4096]{2,1,0:T(8,128)S(1)} %copy-done.2, f32[3,32,4096]{2,1,0:T(8,128)S(1)} %copy-done, f32[3,32,4096]{2,1,0:T(8,128)S(1)} %copy-done.1, f32[32,4096]{1,0:T(8,128)S(1)} %copy-done.3, f32[32,4096]{1,0:T(8,128)S(1)} %bitcast.5, ...), custom_call_target="tpu_custom_call" | custom-call | tf_op jit(solution)/shard_map/final/pallas_call | solution.py:558
Async XLA Ops:
  0.6 31.1 %copy-start = (f32[3,32,4096]{2,1,0:T(8,128)S(1)}, f32[3,32,4096]{2,1,0:T(8,128)}, u32[]{:S(2)}) copy-start(f32[3,32,4096]{2,1,0:T(8,128)} %flow.1) | copy-start | bytes 4718596
  0.6 31.1 %copy-start.1 = (f32[3,32,4096]{2,1,0:T(8,128)S(1)}, f32[3,32,4096]{2,1,0:T(8,128)}, u32[]{:S(2)}) copy-start(f32[3,32,4096]{2,1,0:T(8,128)} %diffusion.1) | copy-start | bytes 4718596
  0.7 31.1 %copy-start.2 = (f32[2,32,4096]{2,1,0:T(8,128)S(1)}, f32[2,32,4096]{2,1,0:T(8,128)}, u32[]{:S(2)}) copy-start(f32[2,32,4096]{2,1,0:T(8,128)} %species.1) | copy-start | bytes 3145732
  0.7 31.1 %copy-start.3 = (f32[32,4096]{1,0:T(8,128)S(1)}, f32[32,4096]{1,0:T(8,128)}, u32[]{:S(2)}) copy-start(f32[32,4096]{1,0:T(8,128)} %inv_volume.1) | copy-start | bytes 1572868
  0.7 31.1 %copy-start.4 = (f32[2]{0:T(128)S(1)}, f32[2]{0:T(128)}, u32[]{:S(2)}) copy-start(f32[2]{0:T(128)} %dif.1) | copy-start | bytes 28

commit v6 on v5

--- a/solution.py
+++ b/solution.py
@@ -322,11 +322,11 @@
     onward_z = [sp_copy(forward.at[q], forward.at[q], 2 * CHUNKS + 1, d) for d in (2, 1, 3)]
     for copy in onward + onward_z:
         copy.start()
-    gather_part(0)
 
     got_b = parcels.reshape(NB * ROWS, 128)
     own_cells = jnp.concatenate([own[:, 8 * r : 8 * r + 1] for r in range(CAP)], axis=0)
     speeds = list(lookups(own_cells, fields, (1, 2, 3)))
+    gather_part(0)
 
     @pl.when(q != 0)
     def _():

time: 36.3 us -> 36.3 us (level)
  no operation moved by 1% of the time
where the time goes in v6:
time: 36.3 us
  Pallas kernels  35.5 us (98%)
  between operations  0.72 us (2%)
    pallas_call x1, Pallas kernels, body(): pl.pallas_call(exchange_kernel, out_shape=(shape(NQ, 8, JK), shape(1024,...  31.1 us
    pallas_call x1, Pallas kernels, body(): pl.pallas_call(final_kernel, out_shape=(shape(2, LAYERS, JK), shape(384,...  4.43 us

profile of v6, /device:TPU:2, one launch (start us, length us, event | category | flops | bytes accessed | tf_op | source)
XLA Modules:
  0.0 36.3 jit_solution(11744451154447573233)
XLA Ops:
  0.6 0.0 copy-start
  0.6 0.0 copy-start.1
  0.7 0.0 copy-start.2
  0.7 0.0 copy-start.3
  0.7 0.0 copy-start.4
  0.7 31.1 %exchange.1 = (f32[4,8,4096]{2,1,0:T(8,128)S(1)}, f32[1024,128]{1,0:T(8,128)S(1)}, f32[8,4096]{1,0:T(8,128)S(1)}, f32[4,16,8,128]{3,2,1,0:T(8,128)S(1)}, f32[384,128]{1,0:T(8,128)S(1)}) custom-call(f32[2]{0:T(128)} %dif.1, f32[2,32,4096]{2,1,0:T(8,128)} %species.1, f32[3,32,4096]{2,1,0:T(8,128)} %flow.1, f32[3,32,4096]{2,1,0:T(8,128)} %diffusion.1, ...), custom_call_target="tpu_custom_call" | custom-call | tf_op jit(solution)/shard_map/exchange/pallas_call | solution.py:538
  31.8 0.0 copy-done
  31.8 0.0 copy-done.1
  31.8 0.0 copy-done.2
  31.8 0.0 copy-done.3
  31.8 0.0 copy-done.4
  31.8 4.4 %final.1 = (f32[2,32,4096]{2,1,0:T(8,128)}, f32[384,128]{1,0:T(8,128)}) custom-call(f32[2]{0:T(128)S(1)} %copy-done.4, f32[2,32,4096]{2,1,0:T(8,128)S(1)} %copy-done.2, f32[3,32,4096]{2,1,0:T(8,128)S(1)} %copy-done, f32[3,32,4096]{2,1,0:T(8,128)S(1)} %copy-done.1, f32[32,4096]{1,0:T(8,128)S(1)} %copy-done.3, f32[32,4096]{1,0:T(8,128)S(1)} %bitcast.5, ...), custom_call_target="tpu_custom_call" | custom-call | tf_op jit(solution)/shard_map/final/pallas_call | solution.py:558
Async XLA Ops:
  0.6 31.1 %copy-start = (f32[3,32,4096]{2,1,0:T(8,128)S(1)}, f32[3,32,4096]{2,1,0:T(8,128)}, u32[]{:S(2)}) copy-start(f32[3,32,4096]{2,1,0:T(8,128)} %flow.1) | copy-start | bytes 4718596
  0.6 31.1 %copy-start.1 = (f32[3,32,4096]{2,1,0:T(8,128)S(1)}, f32[3,32,4096]{2,1,0:T(8,128)}, u32[]{:S(2)}) copy-start(f32[3,32,4096]{2,1,0:T(8,128)} %diffusion.1) | copy-start | bytes 4718596
  0.7 31.1 %copy-start.2 = (f32[2,32,4096]{2,1,0:T(8,128)S(1)}, f32[2,32,4096]{2,1,0:T(8,128)}, u32[]{:S(2)}) copy-start(f32[2,32,4096]{2,1,0:T(8,128)} %species.1) | copy-start | bytes 3145732
  0.7 31.1 %copy-start.3 = (f32[32,4096]{1,0:T(8,128)S(1)}, f32[32,4096]{1,0:T(8,128)}, u32[]{:S(2)}) copy-start(f32[32,4096]{1,0:T(8,128)} %inv_volume.1) | copy-start | bytes 1572868
  0.7 31.1 %copy-start.4 = (f32[2]{0:T(128)S(1)}, f32[2]{0:T(128)}, u32[]{:S(2)}) copy-start(f32[2]{0:T(128)} %dif.1) | copy-start | bytes 28
